TPU v7x, 32 devices: a whole 2x2x4 slice. The times are simulated.
32 devices in a mesh: pole: 4 (over y, x), row: 2 (over core), col: 4 (over z).
Axes of the slice: x: 2, y: 2, z: 4, core: 2. Of those that a mesh axis runs over, the one named last changes fastest.
Arguments:
- ancestor_inverse: bfloat16 [8, 2, 8192, 8192], P('pole', None, 'row', 'col'), may hold values from -0.0625 to 0.0625
- lower_factor: bfloat16 [2, 2, 256, 8192], P(None, None, 'row', 'col'), may hold values from -6 to 6
- upper_factor: bfloat16 [2, 2, 256, 8192], P(None, None, 'col', 'row'), may hold values from -0.0625 to 0.0625
- diag_inverse: float32 [8, 2, 2, 256, 256], P('pole', None, None, 'row', 'col'), may hold values from -6 to 6
- pole_weights: float32 [8, 2], P('pole'), may hold values from -2 to 2
Outputs:
- column_density: float32 [8192, 2, 256], P('row', None, 'col')
- diag_density: float32 [2, 256, 256], P(None, 'row', 'col')
All inputs are finite; a program needn't handle non-finite values.
Results may differ from a plain program's by a relative error of at most 0.0003.
Values may be sent and summed in bfloat16 or wider, within the bound.
No kernel may reach another device: no remote copies, remote signals or barrier semaphores. Data moves between devices by JAX's collectives and lax.ppermute only.
A program may use at most 256 MiB of HBM per device.

v0:
```python
import jax
import jax.numpy as jnp
from jax import lax
from jax.sharding import PartitionSpec as P


def weigh(columns, pole_weights):
    weight_real = pole_weights[:, 0].reshape(-1, 1, 1, 1)
    weight_imag = pole_weights[:, 1].reshape(-1, 1, 1, 1)
    sum_real = jnp.sum(weight_real * columns[:, 0] - weight_imag * columns[:, 1], axis=0)
    sum_imag = jnp.sum(weight_real * columns[:, 1] + weight_imag * columns[:, 0], axis=0)
    return jnp.stack([sum_real, sum_imag], axis=0)


def project(source, piece):
    upper = piece.astype(jnp.float32)
    result = jnp.einsum("nsi,int->nst", upper[:, 0], source[1], precision=lax.Precision.HIGHEST)
    return result + jnp.einsum(
        "nsi,int->nst", upper[:, 1], source[0], precision=lax.Precision.HIGHEST
    )


def per_device(ancestor_inverse, lower_factor, upper_factor, diag_inverse, pole_weights):
    pole_dev, _, rows_local, cols_local = ancestor_inverse.shape
    nodes = lower_factor.shape[0]
    blocks = ancestor_inverse.reshape(pole_dev * 2 * rows_local, cols_local)
    piece = lax.all_gather(lower_factor, "row", axis=2, tiled=True)
    width = piece.shape[2]
    flat = piece.reshape(nodes * 2 * width, cols_local)
    product = lax.dot_general(
        blocks, flat, (((1,), (1,)), ((), ())), preferred_element_type=jnp.float32
    )
    product = product.reshape(pole_dev, 2, rows_local, nodes, 2, width)
    real_part = product[:, 1, :, :, 1] - product[:, 0, :, :, 0]
    imag_part = -(product[:, 0, :, :, 1] + product[:, 1, :, :, 0])
    columns = jnp.stack([real_part, imag_part], axis=1)
    local = lax.psum_scatter(weigh(columns, pole_weights), "col", scatter_dimension=3, tiled=True)
    weight_real = pole_weights[:, 0].reshape(-1, 1, 1, 1)
    weight_imag = pole_weights[:, 1].reshape(-1, 1, 1, 1)
    weighted_diag = jnp.sum(
        weight_real * diag_inverse[:, :, 1] + weight_imag * diag_inverse[:, :, 0], axis=0
    )
    total, diag_total = lax.psum((local, weighted_diag), "pole")
    product = project(total, lax.all_gather(upper_factor, "col", axis=2, tiled=True))
    diag_density = diag_total - lax.psum_scatter(product, "row", scatter_dimension=1, tiled=True)
    return (total[1], diag_density)


def solution(mesh):
    placed = (
        P("pole", None, "row", "col"),
        P(None, None, "row", "col"),
        P(None, None, "col", "row"),
        P("pole", None, None, "row", "col"),
        P("pole", None),
    )
    return jax.shard_map(
        per_device,
        mesh=mesh,
        in_specs=placed,
        out_specs=(P("row", None, "col"), P(None, "row", "col")),
        check_vma=False,
    )
```

profile of v0, /device:TPU:0, one launch (start us, length us, event | category | flops | bytes accessed | tf_op | source)
XLA Modules:
  0.0 734.1 jit_solution(10411746994360747336)
XLA Ops:
  7.2 0.0 all-gather.3.cloned.1.call-start
  7.2 0.7 all-gather.3.cloned.1.call-update
  7.9 0.0 reduce-scatter.3.cloned.1.call-start
  7.9 1.0 slice_reduce_fusion.1
  8.9 17.0 %all-gather.3.cloned.1.call-done = bf16[2,2,256,2048]{3,2,1,0:T(8,128)(2,1)} async-done(((bf16[2,2,128,2048]{3,2,1,0:T(8,128)(2,1)}), bf16[2,2,256,2048]{3,2,1,0:T(8,128)(2,1)}) %all-gather.3.cloned.1.call-update) | async-done | bytes 4194320 | tf_op jit(solution)/shard_map/all_gather | solution.py:27
  25.9 79.4 %fusion = f32[2,2,4096,2,2,256]{5,2,4,3,1,0:T(8,128)} fusion(bf16[2,2,4096,2048]{3,2,1,0:T(8,128)(2,1)} %param.5, bf16[2,2,256,2048]{3,2,1,0:T(8,128)(2,1)} %all-gather.3.cloned.1.call-done), kind=kOutput, calls=%fused_computation | convolution fusion | flops 68719476736 | bytes 138412032 | tf_op jit(solution)/shard_map/dot_general | solution.py:30
  105.3 29.6 %subtract_reduce_fusion = (f32[4096,2,256]{2,0,1:T(8,128)}, f32[4096,2,256]{2,0,1:T(8,128)}) fusion(f32[2]{0:T(128)S(1)} %get-tuple-element.5, f32[2]{0:T(128)S(1)} %get-tuple-element.4, f32[2,2,4096,2,2,256]{5,2,4,3,1,0:T(8,128)} %fusion), kind=kLoop, calls=%fused_computation.11 | loop fusion | flops 41943040 | bytes 83886096 | tf_op jit(solution)/shard_map/reduce_sum | solution.py:10
  134.9 8.9 %copy.13 = f32[4096,2,256]{0,2,1:T(8,128)} copy(f32[4096,2,256]{2,0,1:T(8,128)} %get-tuple-element.2) | data formatting | bytes 16777216 | tf_op jit(solution)/shard_map/reduce_sum | solution.py:10
  143.8 8.9 %copy.14 = f32[4096,2,256]{0,2,1:T(8,128)} copy(f32[4096,2,256]{2,0,1:T(8,128)} %get-tuple-element.3) | data formatting | bytes 16777216 | tf_op jit(solution)/shard_map/reduce_sum | solution.py:11
  152.7 11.6 %pad_maximum_fusion = f32[2,4096,2,256]{1,3,2,0:T(8,128)} fusion(f32[1,4096,2,256]{1,3,2,0:T(8,128)} %bitcast.73, f32[1,4096,2,256]{1,3,2,0:T(8,128)} %bitcast.72), kind=kLoop, calls=%fused_computation.9 | loop fusion | flops 4194304 | bytes 33554432 | tf_op jit(solution)/shard_map/stack | solution.py:12
  164.3 0.0 reduce-scatter.3.cloned.1.call-update
  164.3 0.0 all-reduce.3.cloned.1.call-start
  164.4 0.9 copy-done.2
  165.2 0.7 fusion.12
  166.0 280.1 %reduce-scatter.3.cloned.1.call-done = f32[2,4096,2,64]{1,3,2,0:T(8,128)} async-done(((f32[2,4096,2,256]{1,3,2,0:T(8,128)}), f32[2,4096,2,64]{1,3,2,0:T(8,128)}) %reduce-scatter.3.cloned.1.call-update) | async-done | bytes 4194320 | tf_op jit(solution)/shard_map/reduce_scatter | solution.py:37
  446.1 0.0 all-reduce.3.cloned.1.call-update
  446.1 0.0 all-gather.5.cloned.1.call-start
  446.2 0.0 copy-done.1
  446.2 1.5 copy.16
  447.7 0.0 all-gather.5.cloned.1.call-update
  447.7 0.0 reduce-scatter.5.cloned.1.call-start
  447.7 107.9 %all-reduce.3.cloned.1.call-done = (f32[2,4096,2,64]{1,3,2,0:T(8,128)}, f32[2,128,64]{1,2,0:T(8,128)}) async-done(((f32[2,4096,2,64]{1,3,2,0:T(8,128)}, f32[2,128,64]{1,2,0:T(8,128)}), (f32[2,4096,2,64]{1,3,2,0:T(8,128)}, f32[2,128,64]{1,2,0:T(8,128)})) %all-reduce.3.cloned.1.call-update) | async-done | bytes 4259856 | tf_op jit(solution)/shard_map/psum | solution.py:43
  555.6 1.8 slice_bitcast_fusion.8
  557.4 0.0 copy-start
  557.4 149.3 %all-gather.5.cloned.1.call-done = bf16[2,2,256,4096]{3,2,0,1:T(8,128)(2,1)} async-done(((bf16[2,2,64,4096]{3,2,0,1:T(8,128)(2,1)}), bf16[2,2,256,4096]{3,2,0,1:T(8,128)(2,1)}) %all-gather.5.cloned.1.call-update) | async-done | bytes 8388624 | tf_op jit(solution)/shard_map/all_gather | solution.py:44
  706.7 6.7 fusion.6
  713.4 6.7 fusion.10
  720.1 0.0 reduce-scatter.5.cloned.1.call-update
  720.2 5.9 reduce-scatter.5.cloned.1.call-done
  726.1 0.0 copy-done.3
  726.1 1.5 sub.15
  727.6 0.0 copy-done
  (3 shorter events, 0.0 us)
Async XLA Ops:
  7.2 18.8 %all-gather.3.cloned.1.call-start = ((), (), s32[]{:S(2)}) async-start(), calls=%async_computation.2 | async-start | bytes 6291456 | tf_op jit(solution)/shard_map/all_gather | solution.py:27
  7.9 438.2 %reduce-scatter.3.cloned.1.call-start = ((), (), s32[]{:S(2)}) async-start(), calls=%async_computation.3 | async-start | bytes 20971520 | tf_op jit(solution)/shard_map/reduce_scatter | solution.py:37
  164.3 0.9 copy-start.2
  164.3 281.9 %copy-start.1 = (bf16[2,2,64,4096]{3,2,1,0:T(8,128)(2,1)S(1)}, bf16[2,2,64,4096]{3,2,1,0:T(8,128)(2,1)}, u32[]{:S(2)}) copy-start(bf16[2,2,64,4096]{3,2,1,0:T(8,128)(2,1)} %param.7) | copy-start | bytes 6291460
  164.3 391.3 %all-reduce.3.cloned.1.call-start = ((), (), s32[]{:S(2)}) async-start(), calls=%async_computation.6 | async-start | bytes 8519680 | tf_op jit(solution)/shard_map/psum | solution.py:43
  446.1 260.6 %all-gather.5.cloned.1.call-start = ((), (), s32[]{:S(2)}) async-start(), calls=%async_computation.4 | async-start | bytes 10485760 | tf_op jit(solution)/shard_map/all_gather | solution.py:44
  447.7 278.4 %reduce-scatter.5.cloned.1.call-start = ((), (), s32[]{:S(2)}) async-start(), calls=%async_computation.5 | async-start | bytes 196608 | tf_op jit(solution)/shard_map/reduce_scatter | solution.py:45
  555.6 170.5 %copy-start.3 = (f32[2,128,64]{1,2,0:T(8,128)S(1)}, f32[2,128,64]{1,2,0:T(8,128)}, u32[]{:S(2)}) copy-start(f32[2,128,64]{1,2,0:T(8,128)} %get-tuple-element.7) | copy-start | bytes 196612
  557.4 170.2 %copy-start = (f32[4096,2,64]{0,2,1:T(8,128)}, f32[4096,2,64]{0,2,1:T(8,128)S(1)}, u32[]{:S(2)}) copy-start(f32[4096,2,64]{0,2,1:T(8,128)S(1)} %slice_bitcast_fusion.8) | copy-start | bytes 6291460
Sparse Core Ops, SparseCore 0:
  9.5 16.3 all-gather.2
  164.4 281.6 reduce-scatter.2
  450.2 105.3 all-reduce.2
  557.0 149.5 all-gather.4
  720.3 5.7 reduce-scatter.4
where the time goes:
time: 735 us; the launch traced here: 734 us
  waiting for transfers between devices  561 us (76%)
  matrix products  92.8 us (13%)
  other arithmetic  43.3 us (6%)
  local copies, waits for them, and re-layouts  23 us (3%)
  between operations  13.8 us (2%)
    reduce_scatter x1, waiting for transfers between devices, per_device(): lax.psum_scatter(weigh(columns, pole_weights), 'col', scatter_dimension=3...  280 us
    all_gather x1, waiting for transfers between devices, per_device(): lax.all_gather(upper_factor, 'col', axis=2, tiled=True)  149 us
    psum x1, waiting for transfers between devices, per_device(): total, diag_total = lax.psum((local, weighted_diag), 'pole')  108 us
    dot_general x1, matrix products, per_device(): lax.dot_general(blocks, flat, (((1,), (1,)), ((), ())), preferred_element...  79.4 us
    reduce_sum x1, other arithmetic, weigh(): jnp.sum(weight_real * columns[:, 0] - weight_imag * columns[:, 1], axis=0)  29.6 us
    all_gather x1, waiting for transfers between devices, per_device(): piece = lax.all_gather(lower_factor, 'row', axis=2, tiled=True)  17 us
  transfers between devices with their start and end apart: 5, of which 5 were waited for; matrix products, arithmetic and copies ran while one was open for 1% of the time, Pallas kernels for 0%

commit v1 on v0

v1 whole, which is shorter than its diff:
```python
import functools

import jax
import jax.numpy as jnp
from jax import lax
from jax.experimental import pallas as pl
from jax.experimental.pallas import tpu as pltpu
from jax.sharding import PartitionSpec as P


F32 = jnp.float32
BF16 = jnp.bfloat16
LO = jnp.float8_e4m3fn
LO_FACTOR = jnp.float8_e5m2
SPAN = 250.0
PAD = 16
NT = (((1,), (1,)), ((), ()))


def dot_nt(a, b):
    return lax.dot_general(a, b, NT, preferred_element_type=F32)


def encode(x):
    top = jnp.max(jnp.abs(x), axis=0, keepdims=True)
    scale = (top * 1.01).astype(BF16).astype(F32)
    inverse = jnp.where(scale > 1e-30, SPAN / jnp.maximum(scale, 1e-30), 0.0)
    size = jnp.exp2(jnp.abs(x) * inverse - SPAN / 2)
    code = jnp.where(x < 0, -size, size).astype(BF16)
    return code, jnp.broadcast_to(scale, (PAD, x.shape[1])).astype(BF16)


def decode(payload):
    rows = payload.shape[0] - PAD
    code = payload[:rows].astype(F32)
    scale = payload[rows:].astype(F32)[:1] * (1.0 / SPAN)
    size = (jnp.log2(jnp.abs(code)) + SPAN / 2) * scale
    return jnp.where(code < 0, -size, size)


def write_payload(ref, x):
    rows = x.shape[0]
    code, scale = encode(x)
    ref[:rows] = code
    ref[rows:] = scale


def main_body(outs, steps, halves, nodes, base_ref, w_ref, g_ref, *rest):
    s_ref, s8_ref = rest[:2]
    zr_ref, out_refs = rest[-1 - len(outs)], rest[len(rest) - len(outs) :]
    poles = g_ref.shape[0]
    w_real = w_imag = None
    for p in range(poles):
        a, b = w_ref[2 * p], w_ref[2 * p + 1]
        real, imag = g_ref[p, 0].astype(F32), g_ref[p, 1].astype(F32)
        x, y = a * real - b * imag, a * imag + b * real
        w_real = x if w_real is None else w_real + x
        w_imag = y if w_imag is None else w_imag + y
    hi_real, hi_imag = w_real.astype(BF16), w_imag.astype(BF16)
    lo_real = (w_real - hi_real.astype(F32)).astype(LO)
    lo_imag = (w_imag - hi_imag.astype(F32)).astype(LO)
    back = -w_ref[2 * poles]
    x = dot_nt(s_ref[...], hi_real) + dot_nt(s8_ref[...], lo_real)
    y = dot_nt(s_ref[...], hi_imag) + dot_nt(s8_ref[...], lo_imag)
    half = x.shape[0] // (halves * nodes * 2)
    shape = (halves * nodes, 2, half, x.shape[1])
    x, y = x.reshape(shape), y.reshape(shape)
    flat = (halves * nodes * half, x.shape[3])
    zr_ref[...] = ((x[:, 0] - y[:, 1]) * back).reshape(flat)
    z_imag = ((x[:, 1] + y[:, 0]) * back).reshape(flat)
    if any(outs):
        code, scale = encode(z_imag)
    first = 0
    for remote, count, out_ref in zip(outs, steps, out_refs, strict=True):
        j = pl.program_id(0)

        @pl.when((j >= first) & (j < first + count))
        def _(remote=remote, out_ref=out_ref):
            if remote:
                out_ref[: z_imag.shape[0]] = code
                out_ref[z_imag.shape[0] :] = scale
            else:
                out_ref[...] = z_imag

        first += count


def main_call(outs, widths, halves, nodes, tile, scalars, at, weights, blocks, s, s8, real):
    poles, _, rows, cols = blocks.shape
    flat = s.shape[0] // 2
    steps = [w // tile for w in widths]
    aliased = [] if real is None else [real]
    out_specs, out_shape, first = [], [], 0
    for remote, width, count in zip(outs, widths, steps, strict=True):
        height = flat + PAD if remote else flat
        out_specs.append(
            pl.BlockSpec(
                (height, tile),
                lambda j, b, f=first, n=count: (0, jnp.clip(j - f, 0, n - 1)),
            )
        )
        out_shape.append(jax.ShapeDtypeStruct((height, width), BF16 if remote else F32))
        first += count
    whole = pl.BlockSpec(memory_space=pltpu.VMEM)
    grid_spec = pltpu.PrefetchScalarGridSpec(
        num_scalar_prefetch=1,
        grid=(sum(steps),),
        in_specs=[
            pl.BlockSpec(memory_space=pltpu.SMEM),
            pl.BlockSpec((poles, 2, tile, cols), lambda j, b: (0, 0, b[at + j], 0)),
        ]
        + [whole] * 2
        + [pl.BlockSpec(memory_space=pl.ANY)] * len(aliased),
        out_specs=[pl.BlockSpec((flat, tile), lambda j, b: (0, b[at + j]))] + out_specs,
    )
    return pl.pallas_call(
        functools.partial(main_body, outs, steps, halves, nodes),
        grid_spec=grid_spec,
        out_shape=[jax.ShapeDtypeStruct((flat, rows), F32)] + out_shape,
        input_output_aliases={5: 0} if aliased else {},
        compiler_params=pltpu.CompilerParams(vmem_limit_bytes=44 << 20),
        name="products",
    )(scalars, weights, blocks, s, s8, *aliased)


def pole_body(nodes, per_col, n_in, at, where_ref, own_ref, *rest):
    ins, outs, z_ref = rest[:n_in], rest[n_in:-1], rest[-1]
    z = own_ref[...]
    for ref in ins:
        z = z + decode(ref[...])
    z_ref[...] = z.reshape(z_ref.shape)
    for k, out in enumerate(outs):
        h = where_ref[at + 2 * k]
        first = pl.multiple_of(where_ref[at + 2 * k + 1], per_col)
        part = z_ref[h, :, pl.ds(first, per_col), :]
        part = part.reshape(nodes * per_col, part.shape[2])
        if k:
            write_payload(out, part)
        else:
            out[...] = part


def pole_call(halves, nodes, per_col, n_col, tile, scalars, at, own, received):
    flat, width = own.shape
    block = lambda rows: pl.BlockSpec((rows, tile), lambda j, w: (0, j))
    part = nodes * per_col
    return pl.pallas_call(
        functools.partial(pole_body, nodes, per_col, len(received), at),
        grid_spec=pltpu.PrefetchScalarGridSpec(
            num_scalar_prefetch=1,
            grid=(width // tile,),
            in_specs=[block(flat)] + [block(flat + PAD)] * len(received),
            out_specs=[block(part)] + [block(part + PAD)] * (n_col - 1),
            scratch_shapes=[pltpu.VMEM((halves, nodes, flat // (halves * nodes), tile), F32)],
        ),
        out_shape=[jax.ShapeDtypeStruct((part, width), F32)]
        + [jax.ShapeDtypeStruct((part + PAD, width), BF16)] * (n_col - 1),
        name="pole_sum",
    )(scalars, own, *received)


def col_body(n_in, own_ref, *rest):
    ins, (z_ref, out_ref) = rest[:n_in], rest[n_in:]
    z = own_ref[...]
    for ref in ins:
        z = z + decode(ref[...])
    z_ref[...] = z
    write_payload(out_ref, z)


def col_call(tile, own, received):
    part, width = own.shape
    block = lambda rows: pl.BlockSpec((rows, tile), lambda j: (0, j))
    return pl.pallas_call(
        functools.partial(col_body, len(received)),
        grid=(width // tile,),
        in_specs=[block(part)] + [block(part + PAD)] * len(received),
        out_specs=[block(part), block(part + PAD)],
        out_shape=[
            jax.ShapeDtypeStruct((part, width), F32),
            jax.ShapeDtypeStruct((part + PAD, width), BF16),
        ],
        name="col_sum",
    )(own, *received)


def place_body(n_in, at, at_ref, *rest):
    ins, out_ref, z_ref, sems = rest[:n_in], rest[-3], rest[-2], rest[-1]
    width = z_ref.shape[2]
    copies = []
    for k, ref in enumerate(ins):
        z_ref[k] = decode(ref[...])
        first = pl.multiple_of(at_ref[at + k] * 128, 128)
        copy = pltpu.make_async_copy(z_ref.at[k], out_ref.at[:, pl.ds(first, width)], sems.at[k])
        copy.start()
        copies.append(copy)
    for copy in copies:
        copy.wait()


def place_call(rows, scalars, at, payloads, out):
    part, width = payloads[0].shape[0] - PAD, payloads[0].shape[1]
    n = len(payloads)
    aliased = [] if out is None else [out]
    return pl.pallas_call(
        functools.partial(place_body, n, at),
        in_specs=[pl.BlockSpec(memory_space=pltpu.SMEM)]
        + [pl.BlockSpec(memory_space=pltpu.VMEM)] * n
        + [pl.BlockSpec(memory_space=pl.ANY)] * len(aliased),
        out_specs=pl.BlockSpec(memory_space=pl.ANY),
        out_shape=jax.ShapeDtypeStruct((part, rows), F32),
        scratch_shapes=[pltpu.VMEM((n, part, width), F32), pltpu.SemaphoreType.DMA((n,))],
        input_output_aliases={1 + n: 0} if aliased else {},
        compiler_params=pltpu.CompilerParams(vmem_limit_bytes=16 << 20),
        name="place",
    )(scalars, *payloads, *aliased)


def split(x):
    hi = x.astype(BF16)
    return hi, (x - hi.astype(F32)).astype(BF16)


def project_body(halves, nodes, per_col, n_col, direct, pieces, at, where_ref, z_ref, u_ref, *rest):
    piece_refs, outs, acc_ref = rest[:pieces], rest[pieces : pieces + n_col], rest[-1]
    half = z_ref.shape[0] // (halves * nodes)
    step = pl.program_id(0)

    @pl.when(step == 0)
    def _():
        acc_ref[...] = jnp.zeros_like(acc_ref)

    def add(ref):
        for n in range(nodes):
            rows = [split(z_ref[pl.ds((h * nodes + n) * half, half)]) for h in range(halves)]
            both = jnp.concatenate([x[0] for x in rows] + [x[1] for x in rows], axis=0)
            result = dot_nt(both, ref[n])
            for h in range(halves):
                low = result[(halves + h) * half : (halves + h + 1) * half]
                acc_ref[h, n] += result[h * half : (h + 1) * half] + low

    if pieces:
        pl.when(step < direct)(lambda: add(u_ref))
    else:
        add(u_ref)
    for k, ref in enumerate(piece_refs):
        pl.when(step == direct + k)(functools.partial(add, ref))

    @pl.when(step == pl.num_programs(0) - 1)
    def _():
        for k, out in enumerate(outs):
            if at is None:
                out[...] = acc_ref[0]
                continue
            first = pl.multiple_of(where_ref[at + 2 * k + 1], per_col)
            out[...] = acc_ref[where_ref[at + 2 * k], :, pl.ds(first, per_col), :]


def project_call(halves, nodes, per_col, n_col, tile, scalars, at, order, z, u, u_first, direct, pieces=()):
    flat, rows = z.shape
    size = u.shape[1]
    out = jax.ShapeDtypeStruct((nodes, per_col, size), F32)
    rows_of = (lambda j, w: (0, j)) if order is None else (lambda j, w: (0, w[order + j]))
    return pl.pallas_call(
        functools.partial(project_body, halves, nodes, per_col, n_col, direct, len(pieces), at),
        grid_spec=pltpu.PrefetchScalarGridSpec(
            num_scalar_prefetch=1,
            grid=(rows // tile,),
            in_specs=[
                pl.BlockSpec((flat, tile), rows_of),
                pl.BlockSpec(
                    (nodes, size, tile),
                    lambda j, w: (0, 0, u_first + jnp.minimum(j, direct - 1)),
                ),
            ]
            + [pl.BlockSpec((nodes, size, tile), lambda j, w: (0, 0, 0))] * len(pieces),
            out_specs=[pl.BlockSpec(out.shape, lambda j, w: (0, 0, 0))] * n_col,
            scratch_shapes=[pltpu.VMEM((halves, nodes, flat // (halves * nodes), size), F32)],
        ),
        out_shape=[out] * n_col,
        name="project",
    )(scalars, z, u, *pieces)


def peer(i, k, n):
    return i ^ k if n & (n - 1) == 0 else (i + k) % n


def back_peer(i, k, n):
    return i ^ k if n & (n - 1) == 0 else (i + n - k) % n


def send(x, axis, k, n):
    return lax.ppermute(x, axis, [(i, peer(i, k, n)) for i in range(n)])


def tree_sum(parts):
    while len(parts) > 1:
        parts = [a + b for a, b in zip(parts[::2], parts[1::2], strict=True)]
    return parts[0]


def plan_of(rows, n_pole):
    quarter = rows // n_pole
    if quarter % 1024 == 0 and n_pole == 4:
        widths = [quarter * 3 // 4, quarter // 4]
        calls = [[(0, 3)], [(0, 2), (0, 1)], [(1, 3), (0, 0)], [(1, 2), (1, 1)], [(1, 0)]]
        return widths, calls
    return [quarter], [[(0, k)] for k in reversed(range(n_pole))]


def per_device(sizes, ancestor_inverse, lower_factor, upper_factor, diag_inverse, pole_weights):
    n_pole, n_row, n_col = sizes
    poles, _, rows, cols = ancestor_inverse.shape
    nodes, _, s_row, _ = lower_factor.shape
    size = s_row * n_row
    per_col = size // n_col
    p, r, c = (lax.axis_index(name) for name in ("pole", "row", "col"))

    if n_row == 2:
        halves = 2
        other = lax.ppermute(lower_factor, "row", [(0, 1), (1, 0)])
        s = jnp.stack([lower_factor, other]).reshape(nodes * 2 * size, cols)
    else:
        halves = 1
        s = lax.all_gather(lower_factor, "row", axis=2, tiled=True).reshape(-1, cols)
    s8 = s.astype(LO_FACTOR)
    half = size // halves

    top = jnp.max(jnp.abs(pole_weights)) * poles
    scale = jnp.where(top > 0, 2.0**19 / jnp.maximum(top, 1e-30), 1.0)
    weights = jnp.concatenate([(pole_weights * scale).reshape(-1), (1.0 / scale).reshape(1)])

    quarter = rows // n_pole
    widths, calls = plan_of(rows, n_pole)
    firsts = [sum(widths[:g]) for g in range(len(widths))]
    tile = min(256, *widths)
    part = rows // 2 // n_pole if rows // 2 // n_pole % 512 == 0 else 0
    direct = rows - part * n_pole
    step = min(512, direct)

    numbers, starts = [], []
    for runs in calls:
        starts.append(len(numbers))
        for g, k in runs:
            base = (peer(p, k, n_pole) * quarter + firsts[g]) // tile
            numbers += [base + j for j in range(widths[g] // tile)]
    puts = []
    for first in firsts:
        puts.append(len(numbers))
        numbers += [(back_peer(p, k, n_pole) * quarter + first) // 128 for k in range(n_pole)]
    where = len(numbers)
    for k in range(n_col):
        target = peer(c, k, n_col)
        per_half = half // per_col
        h = target // per_half
        numbers += [h ^ r if halves == 2 else h, target % per_half * per_col]
    order = len(numbers)
    numbers += list(range(direct // step))
    if part:
        numbers += [direct // part + back_peer(p, k, n_pole) for k in range(n_pole)]
    scalars = jnp.stack([jnp.asarray(x, jnp.int32) for x in numbers])

    pieces = []
    if part:
        piece = lax.dynamic_slice_in_dim(upper_factor[:, 1], direct + p * part, part, 2)
        piece = lax.all_gather(piece, "col", axis=1, tiled=True)
        pieces = [piece]
        for k in range(1, n_pole):
            pieces.append(send(piece, "pole", k, n_pole))
    upper_real = lax.dynamic_slice_in_dim(upper_factor[:, 0], p * quarter, quarter, 2)
    upper_real = lax.all_gather(upper_real, "col", axis=1, tiled=True)
    upper_imag = upper_factor[:, 1, :, :direct]
    upper_imag = lax.all_gather(upper_imag, "col", axis=1, tiled=True)

    real = out = None
    shared = []
    done = {g: {} for g in range(len(widths))}
    for i, runs in enumerate(calls):
        real, *results = main_call(
            [k > 0 for _, k in runs], [widths[g] for g, _ in runs], halves, nodes, tile,
            scalars, starts[i], weights, ancestor_inverse, s, s8, real,
        )
        for (g, k), result in zip(runs, results, strict=True):
            if k:
                result = send(result, "pole", k, n_pole)
            done[g][k] = result
        for g, got in done.items():
            if got is None or len(got) < n_pole:
                continue
            done[g] = None
            own, received = got[0], [got[k] for k in range(1, n_pole)]
            own, *parts = pole_call(
                halves, nodes, per_col, n_col, tile, scalars, where, own, received
            )
            received = []
            for k, x in enumerate(parts):
                received.append(send(x, "col", k + 1, n_col))
            total, payload = col_call(tile, own, received)
            payloads = [payload]
            for k in range(1, n_pole):
                payloads.append(send(payload, "pole", k, n_pole))
            out = place_call(rows, scalars, puts[g], payloads, out)
            shared += project_call(
                1, nodes, per_col, 1, tile, scalars, None, None, total, upper_real,
                firsts[g] // tile, widths[g] // tile,
            )

    parts = project_call(
        halves, nodes, per_col, n_col, step, scalars, where, order, real, upper_imag, 0,
        direct // step, pieces,
    )
    shared.append(parts[0])
    for k in range(1, n_col):
        shared.append(send(parts[k], "col", k, n_col))
    shared = sum(shared[1:], shared[0])
    weight_real = pole_weights[:, 0].reshape(-1, 1, 1, 1)
    weight_imag = pole_weights[:, 1].reshape(-1, 1, 1, 1)
    weighted_diag = jnp.sum(
        weight_real * diag_inverse[:, :, 1] + weight_imag * diag_inverse[:, :, 0], axis=0
    ).transpose(0, 2, 1)
    if n_row == 2:
        keep = lax.dynamic_slice_in_dim(shared, r * s_row, s_row, 2)
        give = lax.dynamic_slice_in_dim(shared, (1 - r) * s_row, s_row, 2)
        shared = keep + lax.ppermute(give, "row", [(0, 1), (1, 0)])
    else:
        shared = lax.psum_scatter(shared, "row", scatter_dimension=2, tiled=True)
    mine = weighted_diag - shared
    if n_pole & (n_pole - 1) == 0:
        terms = [mine]
        for k in range(1, n_pole):
            terms.append(send(mine, "pole", k, n_pole))
        diag = tree_sum(terms)
    else:
        diag = lax.psum(mine, "pole")
    density = out.reshape(nodes, per_col, rows).transpose(2, 0, 1)
    return density, diag.transpose(0, 2, 1)


def solution(mesh):
    sizes = tuple(mesh.shape[name] for name in ("pole", "row", "col"))
    placed = (
        P("pole", None, "row", "col"),
        P(None, None, "row", "col"),
        P(None, None, "col", "row"),
        P("pole", None, None, "row", "col"),
        P("pole", None),
    )

    def body(ancestor_inverse, *rest):
        return per_device(sizes, ancestor_inverse, *rest)

    return jax.shard_map(
        body,
        mesh=mesh,
        in_specs=placed,
        out_specs=(P("row", None, "col"), P(None, "row", "col")),
        check_vma=False,
    )
```

time: 735 us -> 246 us (0.33)
  waiting for transfers between devices: 561 us -> 40.6 us
  Pallas kernels: 0 us -> 118 us
  matrix products: 92.8 us -> 0 us
  other arithmetic: 43.3 us -> 6.41 us
  starting transfers between devices: 0.2 us -> 35.5 us
  blocking collectives: 0 us -> 16.4 us
  local copies, waits for them, and re-layouts: 23 us -> 13.4 us
    reduce_scatter x2 -> x0, waiting for transfers between devices: 286 us -> none  [the longest x1 280 us: per_device(): lax.psum_scatter(weigh(columns, pole_weights), 'col', scatter_dimension=3...]
    all_gather x2, waiting for transfers between devices: 166 us -> 0.01 us  [the longest x1 0.01 us: per_device(): upper_imag = lax.all_gather(upper_imag, 'col', axis=1, tiled=True)]
    pallas_call x0 -> x14, Pallas kernels: none -> 118 us  [the longest x5 83.5 us: main_call(): pl.pallas_call(functools.partial(main_body, outs, steps, halves, nodes),...]
    psum x1 -> x0, waiting for transfers between devices: 108 us -> none  [per_device(): total, diag_total = lax.psum((local, weighted_diag), 'pole')]
    dot_general x3 -> x0, matrix products: 92.8 us -> none  [the longest x1 79.4 us: per_device(): lax.dot_general(blocks, flat, (((1,), (1,)), ((), ())), preferred_element...]
    ppermute x0 -> x29, waiting for transfers between devices: none -> 40.5 us  [the longest x27 40.5 us: send(): return lax.ppermute(x, axis, [(i, peer(i, k, n)) for i in range(n)])]
    ppermute x0 -> x29, starting transfers between devices: none -> 35.4 us  [the longest x27 34.7 us: send(): return lax.ppermute(x, axis, [(i, peer(i, k, n)) for i in range(n)])]
    reduce_sum x1 -> x0, other arithmetic: 29.6 us -> none  [weigh(): jnp.sum(weight_real * columns[:, 0] - weight_imag * columns[:, 1], axis=0)]
  transfers between devices with their start and end apart: 5 -> 31, of which waited for: 5 -> 6; matrix products, arithmetic and copies ran while one was open for 1% -> 4% of each run, Pallas kernels for 0% -> 48%
where the time goes in v1:
time: 246 us
  Pallas kernels  118 us (48%)
  waiting for transfers between devices  40.6 us (17%)
  starting transfers between devices  35.5 us (14%)
  blocking collectives  16.4 us (7%)
  between operations  15.4 us (6%)
  local copies, waits for them, and re-layouts  13.4 us (5%)
  other arithmetic  6.41 us (3%)
    pallas_call x5, Pallas kernels, main_call(): pl.pallas_call(functools.partial(main_body, outs, steps, halves, nodes),...  83.5 us
    ppermute x27, waiting for transfers between devices, send(): return lax.ppermute(x, axis, [(i, peer(i, k, n)) for i in range(n)])  40.5 us
    ppermute x27, starting transfers between devices, send(): return lax.ppermute(x, axis, [(i, peer(i, k, n)) for i in range(n)])  34.7 us
    pallas_call x3, Pallas kernels, project_call(): pl.pallas_call(functools.partial(project_body, halves, nodes, per_col, n_...  16.8 us
    all_gather x1, blocking collectives, per_device(): piece = lax.all_gather(piece, 'col', axis=1, tiled=True)  16.4 us
    unnamed x53, local copies, waits for them, and re-layouts  10.1 us
    pallas_call x2, Pallas kernels, pole_call(): pl.pallas_call(functools.partial(pole_body, nodes, per_col, len(received)...  9.4 us
    pallas_call x2, Pallas kernels, col_call(): pl.pallas_call(functools.partial(col_body, len(received)), grid=(width //...  5.03 us
  transfers between devices with their start and end apart: 31, of which 6 were waited for; matrix products, arithmetic and copies ran while one was open for 4% of the time, Pallas kernels for 48%

profile of v1, /device:TPU:0, one launch (start us, length us, event | category | flops | bytes accessed | tf_op | source)
XLA Modules:
  0.0 245.6 jit_solution(15191999206871841001)
XLA Ops:
  7.2 1.9 slice_bitcast_fusion
  9.7 2.8 %fusion.2 = (bf16[2,1,64,4096]{3,2,1,0:T(8,128)(2,1)S(1)}, bf16[2,1,64,4096]{3,2,1,0:T(8,128)(2,1)}) fusion(bf16[2,2,64,4096]{3,2,1,0:T(8,128)(2,1)} %param.7), kind=kLoop, calls=%fused_computation.18 | loop fusion | bytes 4194304 | tf_op jit(solution)/shard_map/slice | solution.py:371
  15.4 2.0 pad_maximum_fusion
  17.4 2.0 bitcast_convert_fusion.rest_1_
  19.4 16.1 %products.5 = (f32[512,4096]{1,0:T(8,128)}, bf16[528,768]{1,0:T(8,128)(2,1)S(1)}) custom-call(s32[40]{0:T(128)S(1)} %stack.156.base_ref.where_ref.at_ref, f32[5]{0:T(128)S(1)} %pad_maximum_fusion.1.w_ref, bf16[2,2,4096,2048]{3,2,1,0:T(8,128)(2,1)} %g_ref.9, bf16[1024,2048]{1,0:T(8,128)(2,1)S(1)} %bitcast.71, ...), custom_call_target="tpu_custom_call" | custom-call | tf_op jit(solution)/shard_map/products/pallas_call | solution.py:116
  35.5 28.4 %products.6 = (f32[512,4096]{1,0:T(8,128)}, bf16[528,768]{1,0:T(8,128)(2,1)}, bf16[528,768]{1,0:T(8,128)(2,1)}) custom-call(s32[40]{0:T(128)S(1)} %stack.156.base_ref.where_ref.at_ref, f32[5]{0:T(128)S(1)} %pad_maximum_fusion.1.w_ref, bf16[2,2,4096,2048]{3,2,1,0:T(8,128)(2,1)} %g_ref.9, ...), custom_call_target="tpu_custom_call", output_to_operand_aliasing={{0}: (5, {})} | custom-call | tf_op jit(solution)/shard_map/products/pallas_call | solution.py:116
  63.9 2.3 collective-permute-start.10
  67.7 2.2 copy-done.1
  69.8 19.9 %products.7 = (f32[512,4096]{1,0:T(8,128)}, bf16[528,256]{1,0:T(8,128)(2,1)S(1)}, f32[512,768]{1,0:T(8,128)S(1)}) custom-call(s32[40]{0:T(128)S(1)} %stack.156.base_ref.where_ref.at_ref, f32[5]{0:T(128)S(1)} %pad_maximum_fusion.1.w_ref, bf16[2,2,4096,2048]{3,2,1,0:T(8,128)(2,1)} %g_ref.9, ...), custom_call_target="tpu_custom_call", output_to_operand_aliasing={{0}: (5, {})} | custom-call | tf_op jit(solution)/shard_map/products/pallas_call | solution.py:116
  89.8 11.7 %products.8 = (f32[512,4096]{1,0:T(8,128)}, bf16[528,256]{1,0:T(8,128)(2,1)S(1)}, bf16[528,256]{1,0:T(8,128)(2,1)S(1)}) custom-call(s32[40]{0:T(128)S(1)} %stack.156.base_ref.where_ref.at_ref, f32[5]{0:T(128)S(1)} %pad_maximum_fusion.1.w_ref, bf16[2,2,4096,2048]{3,2,1,0:T(8,128)(2,1)} %g_ref.9, ...), custom_call_target="tpu_custom_call", output_to_operand_aliasing={{0}: (5, {})} | custom-call | tf_op jit(solution)/shard_map/products/pallas_call | solution.py:116
  101.5 1.9 collective-permute-start.1
  104.3 16.4 %all-gather.2 = bf16[2,1,256,512]{3,2,0,1:T(8,128)(2,1)} all-gather(bf16[2,1,64,512]{3,2,0,1:T(8,128)(2,1)S(1)} %dynamic-slice_bitcast_fusion.1), channel_id=4, replica_groups=mesh['pole'=4,'row'=2,'col'=4] {'col'}, dimensions={2}, use_global_device_ids=true | all-gather | bytes 655360 | tf_op jit(solution)/shard_map/all_gather | solution.py:367
  126.4 5.9 %pole_sum.3 = (f32[128,768]{1,0:T(8,128)}, bf16[144,768]{1,0:T(8,128)(2,1)}, bf16[144,768]{1,0:T(8,128)(2,1)}, bf16[144,768]{1,0:T(8,128)(2,1)}) custom-call(s32[40]{0:T(128)} %copy-done.6, f32[512,768]{1,0:T(8,128)} %copy-done.3, bf16[528,768]{1,0:T(8,128)(2,1)} %collective-permute-done.10.rest_0_, bf16[528,768]{1,0:T(8,128)(2,1)} %collective-permute-done.11.rest_1_, ...), custom_call_target="tpu_custom_call" | custom-call | tf_op jit(solution)/shard_map/pole_sum/pallas_call | solution.py:147
  132.3 23.6 %collective-permute-done.2.rest_1_ = bf16[528,256]{1,0:T(8,128)(2,1)} collective-permute-done((bf16[528,256]{1,0:T(8,128)(2,1)S(1)}, bf16[528,256]{1,0:T(8,128)(2,1)}, u32[]{:S(2)}, u32[]{:S(2)}) %collective-permute-start.2) | collective-permute-done | bytes 270368 | tf_op jit(solution)/shard_map/ppermute | solution.py:294
  155.9 2.2 copy-done.2
  158.0 7.4 %products.9 = (f32[512,4096]{1,0:T(8,128)}, f32[512,256]{1,0:T(8,128)S(1)}) custom-call(s32[40]{0:T(128)S(1)} %copy-done.7, f32[5]{0:T(128)S(1)} %pad_maximum_fusion.1.w_ref, bf16[2,2,4096,2048]{3,2,1,0:T(8,128)(2,1)} %g_ref.9, bf16[1024,2048]{1,0:T(8,128)(2,1)S(1)} %bitcast.75, ...), custom_call_target="tpu_custom_call", output_to_operand_aliasing={{0}: (5, {})} | custom-call | tf_op jit(solution)/shard_map/products/pallas_call | solution.py:116
  167.0 3.5 %pole_sum.2 = (f32[128,256]{1,0:T(8,128)}, bf16[144,256]{1,0:T(8,128)(2,1)}, bf16[144,256]{1,0:T(8,128)(2,1)}, bf16[144,256]{1,0:T(8,128)(2,1)}) custom-call(s32[40]{0:T(128)} %copy-done.6, f32[512,256]{1,0:T(8,128)} %copy-done.4, bf16[528,256]{1,0:T(8,128)(2,1)} %copy-done.12, bf16[528,256]{1,0:T(8,128)(2,1)} %collective-permute-done.2.rest_1_, ...), custom_call_target="tpu_custom_call" | custom-call | tf_op jit(solution)/shard_map/pole_sum/pallas_call | solution.py:147
  170.5 2.0 collective-permute-start.4
  176.3 1.8 collective-permute-done.4.rest_0_
  178.1 2.4 collective-permute-start.6
  180.5 10.3 %project.5 = (f32[2,64,256]{2,1,0:T(8,128)}, f32[2,64,256]{2,1,0:T(8,128)}, f32[2,64,256]{2,1,0:T(8,128)}, f32[2,64,256]{2,1,0:T(8,128)}) custom-call(s32[40]{0:T(128)} %copy-done.6, f32[512,4096]{1,0:T(8,128)} %get-tuple-element.55.z_ref, bf16[2,256,2048]{2,1,0:T(8,128)(2,1)} %bitcast.79, bf16[2,256,512]{2,1,0:T(8,128)(2,1)} %bitcast.47.rest_0_, ...), custom_call_target="tpu_custom_call" | custom-call | tf_op jit(solution)/shard_map/project/pallas_call | solution.py:264
  190.8 5.3 %collective-permute-done.5.rest_1_ = bf16[144,256]{1,0:T(8,128)(2,1)S(1)} collective-permute-done((bf16[144,256]{1,0:T(8,128)(2,1)}, bf16[144,256]{1,0:T(8,128)(2,1)S(1)}, u32[]{:S(2)}, u32[]{:S(2)}) %collective-permute-start.5) | collective-permute-done | bytes 73760 | tf_op jit(solution)/shard_map/ppermute | solution.py:294
  196.1 2.2 collective-permute-start.23
  198.3 2.2 collective-permute-start.24
  200.7 1.9 col_sum.2
  202.5 2.6 %project.4 = f32[2,64,256]{2,1,0:T(8,128)} custom-call(s32[40]{0:T(128)} %copy-done.6, f32[128,256]{1,0:T(8,128)} %get-tuple-element.54.z_ref, bf16[2,256,1024]{2,1,0:T(8,128)(2,1)} %bitcast.77), custom_call_target="tpu_custom_call" | custom-call | tf_op jit(solution)/shard_map/project/pallas_call | solution.py:264
  207.3 3.2 %col_sum.3 = (f32[128,768]{1,0:T(8,128)}, bf16[144,768]{1,0:T(8,128)(2,1)}) custom-call(f32[128,768]{1,0:T(8,128)} %get-tuple-element.48.own_ref, bf16[144,768]{1,0:T(8,128)(2,1)} %copy-done.15, bf16[144,768]{1,0:T(8,128)(2,1)} %copy-done.16, bf16[144,768]{1,0:T(8,128)(2,1)} %copy-done.17), custom_call_target="tpu_custom_call" | custom-call | tf_op jit(solution)/shard_map/col_sum/pallas_call | solution.py:174
  210.5 4.0 %project.3 = f32[2,64,256]{2,1,0:T(8,128)} custom-call(s32[40]{0:T(128)} %copy-done.6, f32[128,768]{1,0:T(8,128)} %get-tuple-element.53.z_ref, bf16[2,256,1024]{2,1,0:T(8,128)(2,1)} %bitcast.78), custom_call_target="tpu_custom_call" | custom-call | tf_op jit(solution)/shard_map/project/pallas_call | solution.py:264
  221.3 5.8 %collective-permute-done.16.rest_1_ = bf16[144,768]{1,0:T(8,128)(2,1)S(1)} collective-permute-done((bf16[144,768]{1,0:T(8,128)(2,1)S(1)}, bf16[144,768]{1,0:T(8,128)(2,1)S(1)}, u32[]{:S(2)}, u32[]{:S(2)}) %collective-permute-start.16) | collective-permute-done | bytes 221216 | tf_op jit(solution)/shard_map/ppermute | solution.py:294
  227.6 2.4 collective-permute-done.17.rest_2_
  230.0 3.0 %collective-permute-start.27 = (f32[2,64,128]{2,1,0:T(8,128)S(1)}, f32[2,64,128]{2,1,0:T(8,128)S(1)}, u32[]{:S(2)}, u32[]{:S(2)}) collective-permute-start(f32[2,64,128]{2,1,0:T(8,128)S(1)} %bitcast_subtract_fusion), channel_id=1, source_target_pairs={{0,16},{8,24},{16,0},{24,8},{1,17},{9,25},{17,1},{25,9},{2,18},{10... | collective-permute-start | bytes 196616 | tf_op jit(solution)/shard_map/ppermute | solution.py:294
  233.2 1.8 place.2.rest_4_
  (114 shorter events, 29.3 us)
Async XLA Ops:
  7.2 173.3 %all-gather.8.cloned.1.call-start = ((), (), s32[]{:S(2)}) async-start(), calls=%async_computation.1 | async-start | bytes 2621440 | tf_op jit(solution)/shard_map/all_gather | solution.py:374
  9.1 193.4 %all-gather.6.cloned.1.call-start = ((), (), s32[]{:S(2)}) async-start(), calls=%async_computation | async-start | bytes 1310720 | tf_op jit(solution)/shard_map/all_gather | solution.py:372
  9.2 6.2 %collective-permute-start = (bf16[2,2,128,2048]{3,2,1,0:T(8,128)(2,1)}, bf16[2,2,128,2048]{3,2,1,0:T(8,128)(2,1)}, u32[]{:S(2)}, u32[]{:S(2)}) collective-permute-start(bf16[2,2,128,2048]{3,2,1,0:T(8,128)(2,1)} %param.6), channel_id=1, source_target_pairs={{0,4},{4,0},{1,5},{5,1},{2,6},{6,2},{3,7},{7,3},{8,12},{12,8},{9,1... | collective-permute-start | bytes 6291464 | tf_op jit(solution)/shard_map/ppermute | solution.py:322
  15.3 74.5 %copy-start.6 = (s32[40]{0:T(128)}, s32[40]{0:T(128)S(1)}, u32[]{:S(2)}) copy-start(s32[40]{0:T(128)S(1)} %stack.156.base_ref.where_ref.at_ref) | copy-start | bytes 484
  63.9 59.0 %collective-permute-start.10 = (bf16[528,768]{1,0:T(8,128)(2,1)}, bf16[528,768]{1,0:T(8,128)(2,1)}, u32[]{:S(2)}, u32[]{:S(2)}) collective-permute-start(bf16[528,768]{1,0:T(8,128)(2,1)} %get-tuple-element.45), channel_id=1, source_target_pairs={{0,8},{8,0},{16,24},{24,16},{1,9},{9,1},{17,25},{25,17},{2,10},{10... | collective-permute-start | bytes 2433032 | tf_op jit(solution)/shard_map/ppermute | solution.py:294
  66.1 58.1 %collective-permute-start.11 = (bf16[528,768]{1,0:T(8,128)(2,1)}, bf16[528,768]{1,0:T(8,128)(2,1)}, u32[]{:S(2)}, u32[]{:S(2)}) collective-permute-start(bf16[528,768]{1,0:T(8,128)(2,1)} %get-tuple-element.46), channel_id=1, source_target_pairs={{0,16},{8,24},{16,0},{24,8},{1,17},{9,25},{17,1},{25,9},{2,18},{10... | collective-permute-start | bytes 2433032 | tf_op jit(solution)/shard_map/ppermute | solution.py:294
  67.6 58.1 %collective-permute-start.12 = (bf16[528,768]{1,0:T(8,128)(2,1)S(1)}, bf16[528,768]{1,0:T(8,128)(2,1)}, u32[]{:S(2)}, u32[]{:S(2)}) collective-permute-start(bf16[528,768]{1,0:T(8,128)(2,1)S(1)} %get-tuple-element.47), channel_id=1, source_target_pairs={{0,24},{8,16},{16,8},{24,0},{1,25},{9,17},{17,9},{25,1},{2,26},{10... | collective-permute-start | bytes 2433032 | tf_op jit(solution)/shard_map/ppermute | solution.py:294
  101.5 19.9 %collective-permute-start.1 = (bf16[528,256]{1,0:T(8,128)(2,1)S(1)}, bf16[528,256]{1,0:T(8,128)(2,1)S(1)}, u32[]{:S(2)}, u32[]{:S(2)}) collective-permute-start(bf16[528,256]{1,0:T(8,128)(2,1)S(1)} %get-tuple-element.36), channel_id=1, source_target_pairs={{0,8},{8,0},{16,24},{24,16},{1,9},{9,1},{17,25},{25,17},{2,10},{10... | collective-permute-start | bytes 811016 | tf_op jit(solution)/shard_map/ppermute | solution.py:294
  120.7 51.7 %collective-permute-start.19 = (bf16[2,256,512]{2,1,0:T(8,128)(2,1)}, bf16[2,256,512]{2,1,0:T(8,128)(2,1)}, u32[]{:S(2)}, u32[]{:S(2)}) collective-permute-start(bf16[2,256,512]{2,1,0:T(8,128)(2,1)} %bitcast.47.rest_0_), channel_id=1, source_target_pairs={{0,8},{8,0},{16,24},{24,16},{1,9},{9,1},{17,25},{25,17},{2,10},{10... | collective-permute-start | bytes 1572872 | tf_op jit(solution)/shard_map/ppermute | solution.py:294
  121.4 52.1 %collective-permute-start.20 = (bf16[2,256,512]{2,1,0:T(8,128)(2,1)}, bf16[2,256,512]{2,1,0:T(8,128)(2,1)}, u32[]{:S(2)}, u32[]{:S(2)}) collective-permute-start(bf16[2,256,512]{2,1,0:T(8,128)(2,1)} %bitcast.47.rest_0_), channel_id=1, source_target_pairs={{0,16},{8,24},{16,0},{24,8},{1,17},{9,25},{17,1},{25,9},{2,18},{10... | collective-permute-start | bytes 1572872 | tf_op jit(solution)/shard_map/ppermute | solution.py:294
  122.8 52.1 %collective-permute-start.21 = (bf16[2,256,512]{2,1,0:T(8,128)(2,1)}, bf16[2,256,512]{2,1,0:T(8,128)(2,1)}, u32[]{:S(2)}, u32[]{:S(2)}) collective-permute-start(bf16[2,256,512]{2,1,0:T(8,128)(2,1)} %bitcast.47.rest_0_), channel_id=1, source_target_pairs={{0,24},{8,16},{16,8},{24,0},{1,25},{9,17},{17,9},{25,1},{2,26},{10... | collective-permute-start | bytes 1572872 | tf_op jit(solution)/shard_map/ppermute | solution.py:294
  124.3 31.6 %collective-permute-start.2 = (bf16[528,256]{1,0:T(8,128)(2,1)S(1)}, bf16[528,256]{1,0:T(8,128)(2,1)}, u32[]{:S(2)}, u32[]{:S(2)}) collective-permute-start(bf16[528,256]{1,0:T(8,128)(2,1)S(1)} %get-tuple-element.37), channel_id=1, source_target_pairs={{0,16},{8,24},{16,0},{24,8},{1,17},{9,25},{17,1},{25,9},{2,18},{10... | collective-permute-start | bytes 811016 | tf_op jit(solution)/shard_map/ppermute | solution.py:294
  125.7 40.5 %collective-permute-start.3 = (bf16[528,256]{1,0:T(8,128)(2,1)S(1)}, bf16[528,256]{1,0:T(8,128)(2,1)S(1)}, u32[]{:S(2)}, u32[]{:S(2)}) collective-permute-start(bf16[528,256]{1,0:T(8,128)(2,1)S(1)} %get-tuple-element.38), channel_id=1, source_target_pairs={{0,24},{8,16},{16,8},{24,0},{1,25},{9,17},{17,9},{25,1},{2,26},{10... | collective-permute-start | bytes 811016 | tf_op jit(solution)/shard_map/ppermute | solution.py:294
  155.8 42.4 %collective-permute-start.13 = (bf16[144,768]{1,0:T(8,128)(2,1)}, bf16[144,768]{1,0:T(8,128)(2,1)S(1)}, u32[]{:S(2)}, u32[]{:S(2)}) collective-permute-start(bf16[144,768]{1,0:T(8,128)(2,1)} %get-tuple-element.49), channel_id=1, source_target_pairs={{0,1},{1,0},{2,3},{3,2},{4,5},{5,4},{6,7},{7,6},{8,9},{9,8},{10,11... | collective-permute-start | bytes 663560 | tf_op jit(solution)/shard_map/ppermute | solution.py:294
  170.5 7.6 %collective-permute-start.4 = (bf16[144,256]{1,0:T(8,128)(2,1)}, bf16[144,256]{1,0:T(8,128)(2,1)S(1)}, u32[]{:S(2)}, u32[]{:S(2)}) collective-permute-start(bf16[144,256]{1,0:T(8,128)(2,1)} %get-tuple-element.40), channel_id=1, source_target_pairs={{0,1},{1,0},{2,3},{3,2},{4,5},{5,4},{6,7},{7,6},{8,9},{9,8},{10,11... | collective-permute-start | bytes 221192 | tf_op jit(solution)/shard_map/ppermute | solution.py:294
  172.5 32.6 %collective-permute-start.14 = (bf16[144,768]{1,0:T(8,128)(2,1)S(1)}, bf16[144,768]{1,0:T(8,128)(2,1)S(1)}, u32[]{:S(2)}, u32[]{:S(2)}) collective-permute-start(bf16[144,768]{1,0:T(8,128)(2,1)S(1)} %copy-done.24), channel_id=1, source_target_pairs={{0,2},{1,3},{2,0},{3,1},{4,6},{5,7},{6,4},{7,5},{8,10},{9,11},{10,... | collective-permute-start | bytes 663560 | tf_op jit(solution)/shard_map/ppermute | solution.py:294
  173.5 33.2 %collective-permute-start.15 = (bf16[144,768]{1,0:T(8,128)(2,1)S(1)}, bf16[144,768]{1,0:T(8,128)(2,1)S(1)}, u32[]{:S(2)}, u32[]{:S(2)}) collective-permute-start(bf16[144,768]{1,0:T(8,128)(2,1)S(1)} %copy-done.23), channel_id=1, source_target_pairs={{0,3},{1,2},{2,1},{3,0},{4,7},{5,6},{6,5},{7,4},{8,11},{9,10},{10,... | collective-permute-start | bytes 663560 | tf_op jit(solution)/shard_map/ppermute | solution.py:294
  174.9 21.1 %collective-permute-start.5 = (bf16[144,256]{1,0:T(8,128)(2,1)}, bf16[144,256]{1,0:T(8,128)(2,1)S(1)}, u32[]{:S(2)}, u32[]{:S(2)}) collective-permute-start(bf16[144,256]{1,0:T(8,128)(2,1)} %get-tuple-element.41), channel_id=1, source_target_pairs={{0,2},{1,3},{2,0},{3,1},{4,6},{5,7},{6,4},{7,5},{8,10},{9,11},{10,... | collective-permute-start | bytes 221192 | tf_op jit(solution)/shard_map/ppermute | solution.py:294
  178.1 18.0 %collective-permute-start.6 = (bf16[144,256]{1,0:T(8,128)(2,1)}, bf16[144,256]{1,0:T(8,128)(2,1)S(1)}, u32[]{:S(2)}, u32[]{:S(2)}) collective-permute-start(bf16[144,256]{1,0:T(8,128)(2,1)} %get-tuple-element.42), channel_id=1, source_target_pairs={{0,3},{1,2},{2,1},{3,0},{4,7},{5,6},{6,5},{7,4},{8,11},{9,10},{10,... | collective-permute-start | bytes 221192 | tf_op jit(solution)/shard_map/ppermute | solution.py:294
  196.1 18.4 %collective-permute-start.22 = (f32[2,64,256]{2,1,0:T(8,128)}, f32[2,64,256]{2,1,0:T(8,128)S(1)}, u32[]{:S(2)}, u32[]{:S(2)}) collective-permute-start(f32[2,64,256]{2,1,0:T(8,128)} %get-tuple-element.57), channel_id=1, source_target_pairs={{0,1},{1,0},{2,3},{3,2},{4,5},{5,4},{6,7},{7,6},{8,9},{9,8},{10,11... | collective-permute-start | bytes 393224 | tf_op jit(solution)/shard_map/ppermute | solution.py:294
  196.1 18.4 %collective-permute-start.23 = (f32[2,64,256]{2,1,0:T(8,128)}, f32[2,64,256]{2,1,0:T(8,128)S(1)}, u32[]{:S(2)}, u32[]{:S(2)}) collective-permute-start(f32[2,64,256]{2,1,0:T(8,128)} %get-tuple-element.58), channel_id=1, source_target_pairs={{0,2},{1,3},{2,0},{3,1},{4,6},{5,7},{6,4},{7,5},{8,10},{9,11},{10,... | collective-permute-start | bytes 393224 | tf_op jit(solution)/shard_map/ppermute | solution.py:294
  198.3 16.2 %collective-permute-start.24 = (f32[2,64,256]{2,1,0:T(8,128)}, f32[2,64,256]{2,1,0:T(8,128)S(1)}, u32[]{:S(2)}, u32[]{:S(2)}) collective-permute-start(f32[2,64,256]{2,1,0:T(8,128)} %get-tuple-element.59), channel_id=1, source_target_pairs={{0,3},{1,2},{2,1},{3,0},{4,7},{5,6},{6,5},{7,4},{8,11},{9,10},{10,... | collective-permute-start | bytes 393224 | tf_op jit(solution)/shard_map/ppermute | solution.py:294
  205.1 14.2 %collective-permute-start.7 = (bf16[144,256]{1,0:T(8,128)(2,1)}, bf16[144,256]{1,0:T(8,128)(2,1)S(1)}, u32[]{:S(2)}, u32[]{:S(2)}) collective-permute-start(bf16[144,256]{1,0:T(8,128)(2,1)} %get-tuple-element.43.rest_0_), channel_id=1, source_target_pairs={{0,8},{8,0},{16,24},{24,16},{1,9},{9,1},{17,25},{25,17},{2,10},{10... | collective-permute-start | bytes 221192 | tf_op jit(solution)/shard_map/ppermute | solution.py:294
  215.5 5.2 %collective-permute-start.25 = (f32[2,64,128]{2,1,0:T(8,128)S(1)}, f32[2,64,128]{2,1,0:T(8,128)S(1)}, u32[]{:S(2)}, u32[]{:S(2)}) collective-permute-start(f32[2,64,128]{2,1,0:T(8,128)S(1)} %constant_dynamic-slice_fusion), channel_id=1, source_target_pairs={{0,4},{4,0},{1,5},{5,1},{2,6},{6,2},{3,7},{7,3},{8,12},{12,8},{9,1... | collective-permute-start | bytes 196616 | tf_op jit(solution)/shard_map/ppermute | solution.py:425
  215.7 19.4 %collective-permute-start.8 = (bf16[144,256]{1,0:T(8,128)(2,1)S(1)}, bf16[144,256]{1,0:T(8,128)(2,1)S(1)}, u32[]{:S(2)}, u32[]{:S(2)}) collective-permute-start(bf16[144,256]{1,0:T(8,128)(2,1)S(1)} %copy-done.9), channel_id=1, source_target_pairs={{0,16},{8,24},{16,0},{24,8},{1,17},{9,25},{17,1},{25,9},{2,18},{10... | collective-permute-start | bytes 221192 | tf_op jit(solution)/shard_map/ppermute | solution.py:294
  217.2 17.9 %collective-permute-start.9 = (bf16[144,256]{1,0:T(8,128)(2,1)S(1)}, bf16[144,256]{1,0:T(8,128)(2,1)S(1)}, u32[]{:S(2)}, u32[]{:S(2)}) collective-permute-start(bf16[144,256]{1,0:T(8,128)(2,1)S(1)} %copy-done.9), channel_id=1, source_target_pairs={{0,24},{8,16},{16,8},{24,0},{1,25},{9,17},{17,9},{25,1},{2,26},{10... | collective-permute-start | bytes 221192 | tf_op jit(solution)/shard_map/ppermute | solution.py:294
  217.8 9.3 %collective-permute-start.16 = (bf16[144,768]{1,0:T(8,128)(2,1)S(1)}, bf16[144,768]{1,0:T(8,128)(2,1)S(1)}, u32[]{:S(2)}, u32[]{:S(2)}) collective-permute-start(bf16[144,768]{1,0:T(8,128)(2,1)S(1)} %copy-done.5), channel_id=1, source_target_pairs={{0,8},{8,0},{16,24},{24,16},{1,9},{9,1},{17,25},{25,17},{2,10},{10... | collective-permute-start | bytes 663560 | tf_op jit(solution)/shard_map/ppermute | solution.py:294
  219.3 10.7 %collective-permute-start.17 = (bf16[144,768]{1,0:T(8,128)(2,1)S(1)}, bf16[144,768]{1,0:T(8,128)(2,1)S(1)}, u32[]{:S(2)}, u32[]{:S(2)}) collective-permute-start(bf16[144,768]{1,0:T(8,128)(2,1)S(1)} %copy-done.5), channel_id=1, source_target_pairs={{0,16},{8,24},{16,0},{24,8},{1,17},{9,25},{17,1},{25,9},{2,18},{10... | collective-permute-start | bytes 663560 | tf_op jit(solution)/shard_map/ppermute | solution.py:294
  220.7 12.3 %collective-permute-start.18 = (bf16[144,768]{1,0:T(8,128)(2,1)S(1)}, bf16[144,768]{1,0:T(8,128)(2,1)S(1)}, u32[]{:S(2)}, u32[]{:S(2)}) collective-permute-start(bf16[144,768]{1,0:T(8,128)(2,1)S(1)} %copy-done.5), channel_id=1, source_target_pairs={{0,24},{8,16},{16,8},{24,0},{1,25},{9,17},{17,9},{25,1},{2,26},{10... | collective-permute-start | bytes 663560 | tf_op jit(solution)/shard_map/ppermute | solution.py:294
  227.1 9.4 %collective-permute-start.26 = (f32[2,64,128]{2,1,0:T(8,128)S(1)}, f32[2,64,128]{2,1,0:T(8,128)S(1)}, u32[]{:S(2)}, u32[]{:S(2)}) collective-permute-start(f32[2,64,128]{2,1,0:T(8,128)S(1)} %bitcast_subtract_fusion), channel_id=1, source_target_pairs={{0,8},{8,0},{16,24},{24,16},{1,9},{9,1},{17,25},{25,17},{2,10},{10... | collective-permute-start | bytes 196616 | tf_op jit(solution)/shard_map/ppermute | solution.py:294
  230.0 6.5 %collective-permute-start.27 = (f32[2,64,128]{2,1,0:T(8,128)S(1)}, f32[2,64,128]{2,1,0:T(8,128)S(1)}, u32[]{:S(2)}, u32[]{:S(2)}) collective-permute-start(f32[2,64,128]{2,1,0:T(8,128)S(1)} %bitcast_subtract_fusion), channel_id=1, source_target_pairs={{0,16},{8,24},{16,0},{24,8},{1,17},{9,25},{17,1},{25,9},{2,18},{10... | collective-permute-start | bytes 196616 | tf_op jit(solution)/shard_map/ppermute | solution.py:294
  233.0 5.2 %collective-permute-start.28 = (f32[2,64,128]{2,1,0:T(8,128)S(1)}, f32[2,64,128]{2,1,0:T(8,128)S(1)}, u32[]{:S(2)}, u32[]{:S(2)}) collective-permute-start(f32[2,64,128]{2,1,0:T(8,128)S(1)} %bitcast_subtract_fusion), channel_id=1, source_target_pairs={{0,24},{8,16},{16,8},{24,0},{1,25},{9,17},{17,9},{25,1},{2,26},{10... | collective-permute-start | bytes 196616 | tf_op jit(solution)/shard_map/ppermute | solution.py:294
  (24 other events, 225.3 us)
Sparse Core Ops, SparseCore 0:
  9.5 48.3 all-gather.7
  59.5 26.7 all-gather.5

commit v2 on v1

--- a/solution.py
+++ b/solution.py
@@ -118,7 +118,7 @@
         grid_spec=grid_spec,
         out_shape=[jax.ShapeDtypeStruct((flat, rows), F32)] + out_shape,
         input_output_aliases={5: 0} if aliased else {},
-        compiler_params=pltpu.CompilerParams(vmem_limit_bytes=44 << 20),
+        compiler_params=pltpu.CompilerParams(vmem_limit_bytes=32 << 20),
         name="products",
     )(scalars, weights, blocks, s, s8, *aliased)
 
@@ -155,33 +155,47 @@
         ),
         out_shape=[jax.ShapeDtypeStruct((part, width), F32)]
         + [jax.ShapeDtypeStruct((part + PAD, width), BF16)] * (n_col - 1),
+        compiler_params=pltpu.CompilerParams(vmem_limit_bytes=16 << 20),
         name="pole_sum",
     )(scalars, own, *received)
 
 
-def col_body(n_in, own_ref, *rest):
-    ins, (z_ref, out_ref) = rest[:n_in], rest[n_in:]
+def col_body(n_in, nodes, own_ref, u_ref, *rest):
+    ins, (shared_ref, out_ref) = rest[:n_in], rest[n_in:]
     z = own_ref[...]
     for ref in ins:
         z = z + decode(ref[...])
-    z_ref[...] = z
     write_payload(out_ref, z)
-
-
-def col_call(tile, own, received):
+    half = z.shape[0] // nodes
+    hi, lo = split(z)
+
+    @pl.when(pl.program_id(0) == 0)
+    def _():
+        shared_ref[...] = jnp.zeros_like(shared_ref)
+
+    for n in range(nodes):
+        rows = slice(n * half, (n + 1) * half)
+        shared_ref[n] += dot_nt(hi[rows], u_ref[n]) + dot_nt(lo[rows], u_ref[n])
+
+
+def col_call(tile, nodes, own, received, u, first):
     part, width = own.shape
+    size = u.shape[1]
     block = lambda rows: pl.BlockSpec((rows, tile), lambda j: (0, j))
+    shared = jax.ShapeDtypeStruct((nodes, part // nodes, size), F32)
     return pl.pallas_call(
-        functools.partial(col_body, len(received)),
+        functools.partial(col_body, len(received), nodes),
         grid=(width // tile,),
-        in_specs=[block(part)] + [block(part + PAD)] * len(received),
-        out_specs=[block(part), block(part + PAD)],
-        out_shape=[
-            jax.ShapeDtypeStruct((part, width), F32),
-            jax.ShapeDtypeStruct((part + PAD, width), BF16),
-        ],
+        in_specs=[
+            block(part),
+            pl.BlockSpec((nodes, size, tile), lambda j: (0, 0, first // tile + j)),
+        ]
+        + [block(part + PAD)] * len(received),
+        out_specs=[pl.BlockSpec(shared.shape, lambda j: (0, 0, 0)), block(part + PAD)],
+        out_shape=[shared, jax.ShapeDtypeStruct((part + PAD, width), BF16)],
+        compiler_params=pltpu.CompilerParams(vmem_limit_bytes=16 << 20),
         name="col_sum",
-    )(own, *received)
+    )(own, u, *received)
 
 
 def place_body(n_in, at, at_ref, *rest):
@@ -221,8 +235,8 @@
     return hi, (x - hi.astype(F32)).astype(BF16)
 
 
-def project_body(halves, nodes, per_col, n_col, direct, pieces, at, where_ref, z_ref, u_ref, *rest):
-    piece_refs, outs, acc_ref = rest[:pieces], rest[pieces : pieces + n_col], rest[-1]
+def project_body(halves, nodes, per_col, n_col, at, where_ref, z_ref, u_ref, *rest):
+    outs, acc_ref = rest[:n_col], rest[-1]
     half = z_ref.shape[0] // (halves * nodes)
     step = pl.program_id(0)
 
@@ -230,56 +244,41 @@
     def _():
         acc_ref[...] = jnp.zeros_like(acc_ref)
 
-    def add(ref):
-        for n in range(nodes):
-            rows = [split(z_ref[pl.ds((h * nodes + n) * half, half)]) for h in range(halves)]
-            both = jnp.concatenate([x[0] for x in rows] + [x[1] for x in rows], axis=0)
-            result = dot_nt(both, ref[n])
-            for h in range(halves):
-                low = result[(halves + h) * half : (halves + h + 1) * half]
-                acc_ref[h, n] += result[h * half : (h + 1) * half] + low
-
-    if pieces:
-        pl.when(step < direct)(lambda: add(u_ref))
-    else:
-        add(u_ref)
-    for k, ref in enumerate(piece_refs):
-        pl.when(step == direct + k)(functools.partial(add, ref))
+    for n in range(nodes):
+        rows = [split(z_ref[pl.ds((h * nodes + n) * half, half)]) for h in range(halves)]
+        both = jnp.concatenate([x[0] for x in rows] + [x[1] for x in rows], axis=0)
+        result = dot_nt(both, u_ref[n])
+        for h in range(halves):
+            low = result[(halves + h) * half : (halves + h + 1) * half]
+            acc_ref[h, n] += result[h * half : (h + 1) * half] + low
 
     @pl.when(step == pl.num_programs(0) - 1)
     def _():
         for k, out in enumerate(outs):
-            if at is None:
-                out[...] = acc_ref[0]
-                continue
             first = pl.multiple_of(where_ref[at + 2 * k + 1], per_col)
             out[...] = acc_ref[where_ref[at + 2 * k], :, pl.ds(first, per_col), :]
 
 
-def project_call(halves, nodes, per_col, n_col, tile, scalars, at, order, z, u, u_first, direct, pieces=()):
+def project_call(halves, nodes, per_col, n_col, tile, scalars, at, z, u):
     flat, rows = z.shape
     size = u.shape[1]
     out = jax.ShapeDtypeStruct((nodes, per_col, size), F32)
-    rows_of = (lambda j, w: (0, j)) if order is None else (lambda j, w: (0, w[order + j]))
     return pl.pallas_call(
-        functools.partial(project_body, halves, nodes, per_col, n_col, direct, len(pieces), at),
+        functools.partial(project_body, halves, nodes, per_col, n_col, at),
         grid_spec=pltpu.PrefetchScalarGridSpec(
             num_scalar_prefetch=1,
             grid=(rows // tile,),
             in_specs=[
-                pl.BlockSpec((flat, tile), rows_of),
-                pl.BlockSpec(
-                    (nodes, size, tile),
-                    lambda j, w: (0, 0, u_first + jnp.minimum(j, direct - 1)),
-                ),
-            ]
-            + [pl.BlockSpec((nodes, size, tile), lambda j, w: (0, 0, 0))] * len(pieces),
+                pl.BlockSpec((flat, tile), lambda j, w: (0, j)),
+                pl.BlockSpec((nodes, size, tile), lambda j, w: (0, 0, j)),
+            ],
             out_specs=[pl.BlockSpec(out.shape, lambda j, w: (0, 0, 0))] * n_col,
             scratch_shapes=[pltpu.VMEM((halves, nodes, flat // (halves * nodes), size), F32)],
         ),
         out_shape=[out] * n_col,
+        compiler_params=pltpu.CompilerParams(vmem_limit_bytes=24 << 20),
         name="project",
-    )(scalars, z, u, *pieces)
+    )(scalars, z, u)
 
 
 def peer(i, k, n):
@@ -335,9 +334,7 @@
     widths, calls = plan_of(rows, n_pole)
     firsts = [sum(widths[:g]) for g in range(len(widths))]
     tile = min(256, *widths)
-    part = rows // 2 // n_pole if rows // 2 // n_pole % 512 == 0 else 0
-    direct = rows - part * n_pole
-    step = min(512, direct)
+    step = min(1024, rows)
 
     numbers, starts = [], []
     for runs in calls:
@@ -355,23 +352,12 @@
         per_half = half // per_col
         h = target // per_half
         numbers += [h ^ r if halves == 2 else h, target % per_half * per_col]
-    order = len(numbers)
-    numbers += list(range(direct // step))
-    if part:
-        numbers += [direct // part + back_peer(p, k, n_pole) for k in range(n_pole)]
     scalars = jnp.stack([jnp.asarray(x, jnp.int32) for x in numbers])
 
-    pieces = []
-    if part:
-        piece = lax.dynamic_slice_in_dim(upper_factor[:, 1], direct + p * part, part, 2)
-        piece = lax.all_gather(piece, "col", axis=1, tiled=True)
-        pieces = [piece]
-        for k in range(1, n_pole):
-            pieces.append(send(piece, "pole", k, n_pole))
+    upper_imag = upper_factor[:, 1]
+    upper_imag = lax.all_gather(upper_imag, "col", axis=1, tiled=True)
     upper_real = lax.dynamic_slice_in_dim(upper_factor[:, 0], p * quarter, quarter, 2)
     upper_real = lax.all_gather(upper_real, "col", axis=1, tiled=True)
-    upper_imag = upper_factor[:, 1, :, :direct]
-    upper_imag = lax.all_gather(upper_imag, "col", axis=1, tiled=True)
 
     real = out = None
     shared = []
@@ -396,19 +382,15 @@
             received = []
             for k, x in enumerate(parts):
                 received.append(send(x, "col", k + 1, n_col))
-            total, payload = col_call(tile, own, received)
+            projected, payload = col_call(tile, nodes, own, received, upper_real, firsts[g])
+            shared.append(projected)
             payloads = [payload]
             for k in range(1, n_pole):
                 payloads.append(send(payload, "pole", k, n_pole))
             out = place_call(rows, scalars, puts[g], payloads, out)
-            shared += project_call(
-                1, nodes, per_col, 1, tile, scalars, None, None, total, upper_real,
-                firsts[g] // tile, widths[g] // tile,
-            )
 
     parts = project_call(
-        halves, nodes, per_col, n_col, step, scalars, where, order, real, upper_imag, 0,
-        direct // step, pieces,
+        halves, nodes, per_col, n_col, step, scalars, where, real, upper_imag
     )
     shared.append(parts[0])
     for k in range(1, n_col):

time: 246 us -> 192 us (0.78)
  Pallas kernels: 118 us -> 96.1 us
  waiting for transfers between devices: 40.6 us -> 21.6 us
  blocking collectives: 16.4 us -> 0 us
    ppermute x27 -> x24, waiting for transfers between devices: 40.5 us -> 20.3 us  [send(): return lax.ppermute(x, axis, [(i, peer(i, k, n)) for i in range(n)])]
    all_gather x1 -> x0, blocking collectives: 16.4 us -> none  [per_device(): piece = lax.all_gather(piece, 'col', axis=1, tiled=True)]
    pallas_call x3 -> x1, Pallas kernels: 16.8 us -> 4.52 us  [project_call(): pl.pallas_call(functools.partial(project_body, halves, nodes, per_col, n_...]
    unnamed x53 -> x16, local copies, waits for them, and re-layouts: 10.1 us -> 14.7 us
    pallas_call x2, Pallas kernels: 9.4 us -> 5.4 us  [pole_call(): pl.pallas_call(functools.partial(pole_body, nodes, per_col, len(received)...]
    pallas_call x2, Pallas kernels: 5.03 us -> 2.09 us  [col_call(): pl.pallas_call(functools.partial(col_body, len(received), nodes), grid=(w...]
    slice x1 -> x0, local copies, waits for them, and re-layouts: 2.83 us -> none  [per_device(): upper_factor[:, 0]]
    pallas_call x5, Pallas kernels: 83.5 us -> 80.9 us  [main_call(): pl.pallas_call(functools.partial(main_body, outs, steps, halves, nodes),...]
  transfers between devices with their start and end apart: 31 -> 28, of which waited for: 6 -> 8; matrix products, arithmetic and copies ran while one was open for 4% -> 3% of each run, Pallas kernels for 48% -> 50%
where the time goes in v2:
time: 192 us
  Pallas kernels  96.1 us (50%)
  starting transfers between devices  37.3 us (19%)
  waiting for transfers between devices  21.6 us (11%)
  between operations  15.5 us (8%)
  local copies, waits for them, and re-layouts  15.1 us (8%)
  other arithmetic  6.15 us (3%)
    pallas_call x5, Pallas kernels, main_call(): pl.pallas_call(functools.partial(main_body, outs, steps, halves, nodes),...  80.9 us
    ppermute x24, starting transfers between devices, send(): return lax.ppermute(x, axis, [(i, peer(i, k, n)) for i in range(n)])  36.6 us
    ppermute x24, waiting for transfers between devices, send(): return lax.ppermute(x, axis, [(i, peer(i, k, n)) for i in range(n)])  20.3 us
    unnamed x16, local copies, waits for them, and re-layouts  14.7 us
    pallas_call x2, Pallas kernels, pole_call(): pl.pallas_call(functools.partial(pole_body, nodes, per_col, len(received)...  5.4 us
    pallas_call x1, Pallas kernels, project_call(): pl.pallas_call(functools.partial(project_body, halves, nodes, per_col, n_...  4.52 us
  transfers between devices with their start and end apart: 28, of which 8 were waited for; matrix products, arithmetic and copies ran while one was open for 3% of the time, Pallas kernels for 50%

profile of v2, /device:TPU:0, one launch (start us, length us, event | category | flops | bytes accessed | tf_op | source)
XLA Modules:
  0.0 191.8 jit_solution(3087301881217888579)
XLA Ops:
  7.2 2.7 %slice_bitcast_fusion = (bf16[2,1,64,4096]{3,2,0,1:T(8,128)(2,1)}, bf16[2,1,64,4096]{3,2,1,0:T(8,128)(2,1)S(1)}) fusion(bf16[2,2,64,4096]{3,2,1,0:T(8,128)(2,1)} %param.7), kind=kLoop, calls=%fused_computation.1 | loop fusion | bytes 4194304
  14.7 2.6 %pad_maximum_fusion = bf16[2,2,2,128,2048]{4,3,2,1,0:T(8,128)(2,1)S(1)} fusion(bf16[1,2,2,128,2048]{4,3,2,1,0:T(8,128)(2,1)} %bitcast.34, bf16[1,2,2,128,2048]{4,3,2,1,0:T(8,128)(2,1)} %bitcast.33), kind=kLoop, calls=%fused_computation | loop fusion | flops 2097152 | bytes 8388608 | tf_op jit(solution)/shard_map/stack | solution.py:322
  17.3 2.0 %bitcast_convert_fusion.rest_1_ = f8e5m2[1024,2048]{1,0:T(32,128)(4,1)S(1)} fusion(bf16[2,2,2,128,2048]{4,3,2,1,0:T(8,128)(2,1)S(1)} %pad_maximum_fusion), kind=kLoop, calls=%fused_computation.16 | loop fusion | flops 2097152 | bytes 6291456 | tf_op jit(solution)/shard_map/convert_element_type | solution.py:326
  19.3 15.6 %products.5 = (f32[512,4096]{1,0:T(8,128)S(1)}, bf16[528,768]{1,0:T(8,128)(2,1)S(1)}) custom-call(s32[32]{0:T(128)S(1)} %stack.140.base_ref.where_ref.at_ref, f32[5]{0:T(128)S(1)} %pad_maximum_fusion.1.w_ref, bf16[2,2,4096,2048]{3,2,1,0:T(8,128)(2,1)} %g_ref.9, bf16[1024,2048]{1,0:T(8,128)(2,1)S(1)} %bitcast.63, ...), custom_call_target="tpu_custom_call" | custom-call | tf_op jit(solution)/shard_map/products/pallas_call | solution.py:116
  34.9 27.9 %products.6 = (f32[512,4096]{1,0:T(8,128)S(1)}, bf16[528,768]{1,0:T(8,128)(2,1)S(1)}, bf16[528,768]{1,0:T(8,128)(2,1)S(1)}) custom-call(s32[32]{0:T(128)S(1)} %stack.140.base_ref.where_ref.at_ref, f32[5]{0:T(128)S(1)} %pad_maximum_fusion.1.w_ref, bf16[2,2,4096,2048]{3,2,1,0:T(8,128)(2,1)} %g_ref.9, ...), custom_call_target="tpu_custom_call", output_to_operand_aliasing={{0}: (5, {})} | custom-call | tf_op jit(solution)/shard_map/products/pallas_call | solution.py:116
  62.8 2.8 %collective-permute-start.10 = (bf16[528,768]{1,0:T(8,128)(2,1)S(1)}, bf16[528,768]{1,0:T(8,128)(2,1)S(1)}, u32[]{:S(2)}, u32[]{:S(2)}) collective-permute-start(bf16[528,768]{1,0:T(8,128)(2,1)S(1)} %get-tuple-element.45), channel_id=1, source_target_pairs={{0,8},{8,0},{16,24},{24,16},{1,9},{9,1},{17,25},{25,17},{2,10},{10... | collective-permute-start | bytes 2433032 | tf_op jit(solution)/shard_map/ppermute | solution.py:293
  65.6 1.5 collective-permute-start.11
  67.2 19.7 %products.7 = (f32[512,4096]{1,0:T(8,128)S(1)}, bf16[528,256]{1,0:T(8,128)(2,1)S(1)}, f32[512,768]{1,0:T(8,128)S(1)}) custom-call(s32[32]{0:T(128)S(1)} %stack.140.base_ref.where_ref.at_ref, f32[5]{0:T(128)S(1)} %pad_maximum_fusion.1.w_ref, bf16[2,2,4096,2048]{3,2,1,0:T(8,128)(2,1)} %g_ref.9, ...), custom_call_target="tpu_custom_call", output_to_operand_aliasing={{0}: (5, {})} | custom-call | tf_op jit(solution)/shard_map/products/pallas_call | solution.py:116
  86.9 11.0 %products.8 = (f32[512,4096]{1,0:T(8,128)S(1)}, bf16[528,256]{1,0:T(8,128)(2,1)S(1)}, bf16[528,256]{1,0:T(8,128)(2,1)S(1)}) custom-call(s32[32]{0:T(128)S(1)} %stack.140.base_ref.where_ref.at_ref, f32[5]{0:T(128)S(1)} %pad_maximum_fusion.1.w_ref, bf16[2,2,4096,2048]{3,2,1,0:T(8,128)(2,1)} %g_ref.9, ...), custom_call_target="tpu_custom_call", output_to_operand_aliasing={{0}: (5, {})} | custom-call | tf_op jit(solution)/shard_map/products/pallas_call | solution.py:116
  97.9 2.0 %collective-permute-start.1 = (bf16[528,256]{1,0:T(8,128)(2,1)S(1)}, bf16[528,256]{1,0:T(8,128)(2,1)S(1)}, u32[]{:S(2)}, u32[]{:S(2)}) collective-permute-start(bf16[528,256]{1,0:T(8,128)(2,1)S(1)} %get-tuple-element.36), channel_id=1, source_target_pairs={{0,8},{8,0},{16,24},{24,16},{1,9},{9,1},{17,25},{25,17},{2,10},{10... | collective-permute-start | bytes 811016 | tf_op jit(solution)/shard_map/ppermute | solution.py:293
  99.9 1.5 collective-permute-start.2
  103.5 3.9 %pole_sum.3 = (f32[128,768]{1,0:T(8,128)S(1)}, bf16[144,768]{1,0:T(8,128)(2,1)S(1)}, bf16[144,768]{1,0:T(8,128)(2,1)S(1)}, bf16[144,768]{1,0:T(8,128)(2,1)S(1)}) custom-call(s32[32]{0:T(128)S(1)} %stack.140.base_ref.where_ref.at_ref, f32[512,768]{1,0:T(8,128)S(1)} %get-tuple-element.44.own_ref, bf16[528,768]{1,0:T(8,128)(2,1)S(1)} %collective-permute-done.10.rest_0_, ...), custom_call_target="tpu_custom_call" | custom-call | tf_op jit(solution)/shard_map/pole_sum/pallas_call | solution.py:147
  107.4 1.6 collective-permute-start.13
  109.0 6.7 %products.9 = (f32[512,4096]{1,0:T(8,128)S(1)}, f32[512,256]{1,0:T(8,128)S(1)}) custom-call(s32[32]{0:T(128)S(1)} %stack.140.base_ref.where_ref.at_ref, f32[5]{0:T(128)S(1)} %pad_maximum_fusion.1.w_ref, bf16[2,2,4096,2048]{3,2,1,0:T(8,128)(2,1)} %g_ref.9, bf16[1024,2048]{1,0:T(8,128)(2,1)S(1)} %bitcast.67, ...), custom_call_target="tpu_custom_call", output_to_operand_aliasing={{0}: (5, {})} | custom-call | tf_op jit(solution)/shard_map/products/pallas_call | solution.py:116
  115.7 3.3 %copy-done = f32[512,4096]{1,0:T(8,128)} copy-done((f32[512,4096]{1,0:T(8,128)}, f32[512,4096]{1,0:T(8,128)S(1)}, u32[]{:S(2)}) %copy-start) | copy-done | bytes 8388632
  121.0 2.6 %collective-permute-start.14 = (bf16[144,768]{1,0:T(8,128)(2,1)S(1)}, bf16[144,768]{1,0:T(8,128)(2,1)S(1)}, u32[]{:S(2)}, u32[]{:S(2)}) collective-permute-start(bf16[144,768]{1,0:T(8,128)(2,1)S(1)} %get-tuple-element.50), channel_id=1, source_target_pairs={{0,2},{1,3},{2,0},{3,1},{4,6},{5,7},{6,4},{7,5},{8,10},{9,11},{10,... | collective-permute-start | bytes 663560 | tf_op jit(solution)/shard_map/ppermute | solution.py:293
  124.9 1.7 collective-permute-start.5
  126.6 3.4 %collective-permute-done.4.rest_0_ = bf16[144,256]{1,0:T(8,128)(2,1)S(1)} collective-permute-done((bf16[144,256]{1,0:T(8,128)(2,1)S(1)}, bf16[144,256]{1,0:T(8,128)(2,1)S(1)}, u32[]{:S(2)}, u32[]{:S(2)}) %collective-permute-start.4) | collective-permute-done | bytes 73760 | tf_op jit(solution)/shard_map/ppermute | solution.py:293
  131.4 3.4 %copy-done.1 = f32[512,4096]{1,0:T(8,128)S(1)} copy-done((f32[512,4096]{1,0:T(8,128)S(1)}, f32[512,4096]{1,0:T(8,128)}, u32[]{:S(2)}) %copy-start.1) | copy-done | bytes 8388632
  134.8 2.2 %copy-done.2 = bf16[2,1,256,4096]{3,2,0,1:T(8,128)(2,1)S(1)} copy-done((bf16[2,1,256,4096]{3,2,0,1:T(8,128)(2,1)S(1)}, bf16[2,1,256,4096]{3,2,0,1:T(8,128)(2,1)}, u32[]{:S(2)}) %copy-start.2) | copy-done | bytes 4194328
  136.9 4.5 %project.1 = (f32[2,64,256]{2,1,0:T(8,128)S(1)}, f32[2,64,256]{2,1,0:T(8,128)S(1)}, f32[2,64,256]{2,1,0:T(8,128)S(1)}, f32[2,64,256]{2,1,0:T(8,128)S(1)}) custom-call(s32[32]{0:T(128)S(1)} %stack.140.base_ref.where_ref.at_ref, f32[512,4096]{1,0:T(8,128)S(1)} %copy-done.1, bf16[2,256,4096]{2,1,0:T(8,128)(2,1)S(1)} %bitcast.68), custom_call_target="tpu_custom_call" | custom-call | tf_op jit(solution)/shard_map/project/pallas_call | solution.py:266
  141.5 8.8 %collective-permute-done.5.rest_1_ = bf16[144,256]{1,0:T(8,128)(2,1)S(1)} collective-permute-done((bf16[144,256]{1,0:T(8,128)(2,1)S(1)}, bf16[144,256]{1,0:T(8,128)(2,1)S(1)}, u32[]{:S(2)}, u32[]{:S(2)}) %collective-permute-start.5) | collective-permute-done | bytes 73760 | tf_op jit(solution)/shard_map/ppermute | solution.py:293
  150.2 2.1 %collective-permute-start.20 = (f32[2,64,256]{2,1,0:T(8,128)S(1)}, f32[2,64,256]{2,1,0:T(8,128)S(1)}, u32[]{:S(2)}, u32[]{:S(2)}) collective-permute-start(f32[2,64,256]{2,1,0:T(8,128)S(1)} %get-tuple-element.58), channel_id=1, source_target_pairs={{0,2},{1,3},{2,0},{3,1},{4,6},{5,7},{6,4},{7,5},{8,10},{9,11},{10,... | collective-permute-start | bytes 393224 | tf_op jit(solution)/shard_map/ppermute | solution.py:293
  152.3 2.3 %collective-permute-start.21 = (f32[2,64,256]{2,1,0:T(8,128)S(1)}, f32[2,64,256]{2,1,0:T(8,128)S(1)}, u32[]{:S(2)}, u32[]{:S(2)}) collective-permute-start(f32[2,64,256]{2,1,0:T(8,128)S(1)} %get-tuple-element.59), channel_id=1, source_target_pairs={{0,3},{1,2},{2,1},{3,0},{4,7},{5,6},{6,5},{7,4},{8,11},{9,10},{10,... | collective-permute-start | bytes 393224 | tf_op jit(solution)/shard_map/ppermute | solution.py:293
  159.2 1.8 col_sum.3
  163.3 1.8 collective-permute-start.9
  166.8 1.8 collective-permute-start.18
  168.6 4.8 %collective-permute-done.16.rest_1_ = bf16[144,768]{1,0:T(8,128)(2,1)S(1)} collective-permute-done((bf16[144,768]{1,0:T(8,128)(2,1)S(1)}, bf16[144,768]{1,0:T(8,128)(2,1)S(1)}, u32[]{:S(2)}, u32[]{:S(2)}) %collective-permute-start.16) | collective-permute-done | bytes 221216 | tf_op jit(solution)/shard_map/ppermute | solution.py:293
  173.4 1.6 collective-permute-start.23
  175.0 3.6 %collective-permute-start.24 = (f32[2,64,128]{2,1,0:T(8,128)S(1)}, f32[2,64,128]{2,1,0:T(8,128)S(1)}, u32[]{:S(2)}, u32[]{:S(2)}) collective-permute-start(f32[2,64,128]{2,1,0:T(8,128)S(1)} %bitcast_subtract_fusion), channel_id=1, source_target_pairs={{0,16},{8,24},{16,0},{24,8},{1,17},{9,25},{17,1},{25,9},{2,18},{10... | collective-permute-start | bytes 196616 | tf_op jit(solution)/shard_map/ppermute | solution.py:293
  178.9 2.1 %collective-permute-start.25 = (f32[2,64,128]{2,1,0:T(8,128)S(1)}, f32[2,64,128]{2,1,0:T(8,128)S(1)}, u32[]{:S(2)}, u32[]{:S(2)}) collective-permute-start(f32[2,64,128]{2,1,0:T(8,128)S(1)} %bitcast_subtract_fusion), channel_id=1, source_target_pairs={{0,24},{8,16},{16,8},{24,0},{1,25},{9,17},{17,9},{25,1},{2,26},{10... | collective-permute-start | bytes 196616 | tf_op jit(solution)/shard_map/ppermute | solution.py:293
  181.0 1.8 place.2.rest_4_
  (67 shorter events, 21.3 us)
Async XLA Ops:
  7.2 4.5 %copy-start.6 = (f32[2,2]{1,0:T(2,128)S(1)}, f32[2,2]{1,0:T(2,128)}, u32[]{:S(2)}) copy-start(f32[2,2]{1,0:T(2,128)} %param.9) | copy-start | bytes 52
  7.2 124.2 %all-gather.7.cloned.1.call-start = ((), (), s32[]{:S(2)}) async-start(), calls=%async_computation.1 | async-start | bytes 5242880 | tf_op jit(solution)/shard_map/all_gather | solution.py:358
  9.9 144.9 %all-gather.5.cloned.1.call-start = ((), (), s32[]{:S(2)}) async-start(), calls=%async_computation | async-start | bytes 1310720 | tf_op jit(solution)/shard_map/all_gather | solution.py:360
  10.0 4.7 %collective-permute-start = (bf16[2,2,128,2048]{3,2,1,0:T(8,128)(2,1)}, bf16[2,2,128,2048]{3,2,1,0:T(8,128)(2,1)}, u32[]{:S(2)}, u32[]{:S(2)}) collective-permute-start(bf16[2,2,128,2048]{3,2,1,0:T(8,128)(2,1)} %param.6), channel_id=1, source_target_pairs={{0,4},{4,0},{1,5},{5,1},{2,6},{6,2},{3,7},{7,3},{8,12},{12,8},{9,1... | collective-permute-start | bytes 6291464 | tf_op jit(solution)/shard_map/ppermute | solution.py:321
  62.8 38.7 %collective-permute-start.10 = (bf16[528,768]{1,0:T(8,128)(2,1)S(1)}, bf16[528,768]{1,0:T(8,128)(2,1)S(1)}, u32[]{:S(2)}, u32[]{:S(2)}) collective-permute-start(bf16[528,768]{1,0:T(8,128)(2,1)S(1)} %get-tuple-element.45), channel_id=1, source_target_pairs={{0,8},{8,0},{16,24},{24,16},{1,9},{9,1},{17,25},{25,17},{2,10},{10... | collective-permute-start | bytes 2433032 | tf_op jit(solution)/shard_map/ppermute | solution.py:293
  65.6 37.4 %collective-permute-start.11 = (bf16[528,768]{1,0:T(8,128)(2,1)S(1)}, bf16[528,768]{1,0:T(8,128)(2,1)S(1)}, u32[]{:S(2)}, u32[]{:S(2)}) collective-permute-start(bf16[528,768]{1,0:T(8,128)(2,1)S(1)} %get-tuple-element.46), channel_id=1, source_target_pairs={{0,16},{8,24},{16,0},{24,8},{1,17},{9,25},{17,1},{25,9},{2,18},{10... | collective-permute-start | bytes 2433032 | tf_op jit(solution)/shard_map/ppermute | solution.py:293
  67.2 36.3 %collective-permute-start.12 = (bf16[528,768]{1,0:T(8,128)(2,1)S(1)}, bf16[528,768]{1,0:T(8,128)(2,1)S(1)}, u32[]{:S(2)}, u32[]{:S(2)}) collective-permute-start(bf16[528,768]{1,0:T(8,128)(2,1)S(1)} %get-tuple-element.47), channel_id=1, source_target_pairs={{0,24},{8,16},{16,8},{24,0},{1,25},{9,17},{17,9},{25,1},{2,26},{10... | collective-permute-start | bytes 2433032 | tf_op jit(solution)/shard_map/ppermute | solution.py:293
  97.9 21.1 %collective-permute-start.1 = (bf16[528,256]{1,0:T(8,128)(2,1)S(1)}, bf16[528,256]{1,0:T(8,128)(2,1)S(1)}, u32[]{:S(2)}, u32[]{:S(2)}) collective-permute-start(bf16[528,256]{1,0:T(8,128)(2,1)S(1)} %get-tuple-element.36), channel_id=1, source_target_pairs={{0,8},{8,0},{16,24},{24,16},{1,9},{9,1},{17,25},{25,17},{2,10},{10... | collective-permute-start | bytes 811016 | tf_op jit(solution)/shard_map/ppermute | solution.py:293
  99.9 19.1 %collective-permute-start.2 = (bf16[528,256]{1,0:T(8,128)(2,1)S(1)}, bf16[528,256]{1,0:T(8,128)(2,1)S(1)}, u32[]{:S(2)}, u32[]{:S(2)}) collective-permute-start(bf16[528,256]{1,0:T(8,128)(2,1)S(1)} %get-tuple-element.37), channel_id=1, source_target_pairs={{0,16},{8,24},{16,0},{24,8},{1,17},{9,25},{17,1},{25,9},{2,18},{10... | collective-permute-start | bytes 811016 | tf_op jit(solution)/shard_map/ppermute | solution.py:293
  101.4 17.6 %collective-permute-start.3 = (bf16[528,256]{1,0:T(8,128)(2,1)S(1)}, bf16[528,256]{1,0:T(8,128)(2,1)S(1)}, u32[]{:S(2)}, u32[]{:S(2)}) collective-permute-start(bf16[528,256]{1,0:T(8,128)(2,1)S(1)} %get-tuple-element.38), channel_id=1, source_target_pairs={{0,24},{8,16},{16,8},{24,0},{1,25},{9,17},{17,9},{25,1},{2,26},{10... | collective-permute-start | bytes 811016 | tf_op jit(solution)/shard_map/ppermute | solution.py:293
  107.4 44.9 %collective-permute-start.13 = (bf16[144,768]{1,0:T(8,128)(2,1)S(1)}, bf16[144,768]{1,0:T(8,128)(2,1)S(1)}, u32[]{:S(2)}, u32[]{:S(2)}) collective-permute-start(bf16[144,768]{1,0:T(8,128)(2,1)S(1)} %get-tuple-element.49), channel_id=1, source_target_pairs={{0,1},{1,0},{2,3},{3,2},{4,5},{5,4},{6,7},{7,6},{8,9},{9,8},{10,11... | collective-permute-start | bytes 663560 | tf_op jit(solution)/shard_map/ppermute | solution.py:293
  115.7 3.3 %copy-start = (f32[512,4096]{1,0:T(8,128)}, f32[512,4096]{1,0:T(8,128)S(1)}, u32[]{:S(2)}) copy-start(f32[512,4096]{1,0:T(8,128)S(1)} %get-tuple-element.55.z_ref) | copy-start | bytes 25165828
  120.5 9.5 %collective-permute-start.4 = (bf16[144,256]{1,0:T(8,128)(2,1)S(1)}, bf16[144,256]{1,0:T(8,128)(2,1)S(1)}, u32[]{:S(2)}, u32[]{:S(2)}) collective-permute-start(bf16[144,256]{1,0:T(8,128)(2,1)S(1)} %get-tuple-element.40), channel_id=1, source_target_pairs={{0,1},{1,0},{2,3},{3,2},{4,5},{5,4},{6,7},{7,6},{8,9},{9,8},{10,11... | collective-permute-start | bytes 221192 | tf_op jit(solution)/shard_map/ppermute | solution.py:293
  121.0 35.4 %collective-permute-start.14 = (bf16[144,768]{1,0:T(8,128)(2,1)S(1)}, bf16[144,768]{1,0:T(8,128)(2,1)S(1)}, u32[]{:S(2)}, u32[]{:S(2)}) collective-permute-start(bf16[144,768]{1,0:T(8,128)(2,1)S(1)} %get-tuple-element.50), channel_id=1, source_target_pairs={{0,2},{1,3},{2,0},{3,1},{4,6},{5,7},{6,4},{7,5},{8,10},{9,11},{10,... | collective-permute-start | bytes 663560 | tf_op jit(solution)/shard_map/ppermute | solution.py:293
  123.6 34.3 %collective-permute-start.15 = (bf16[144,768]{1,0:T(8,128)(2,1)S(1)}, bf16[144,768]{1,0:T(8,128)(2,1)S(1)}, u32[]{:S(2)}, u32[]{:S(2)}) collective-permute-start(bf16[144,768]{1,0:T(8,128)(2,1)S(1)} %get-tuple-element.51), channel_id=1, source_target_pairs={{0,3},{1,2},{2,1},{3,0},{4,7},{5,6},{6,5},{7,4},{8,11},{9,10},{10,... | collective-permute-start | bytes 663560 | tf_op jit(solution)/shard_map/ppermute | solution.py:293
  124.9 25.3 %collective-permute-start.5 = (bf16[144,256]{1,0:T(8,128)(2,1)S(1)}, bf16[144,256]{1,0:T(8,128)(2,1)S(1)}, u32[]{:S(2)}, u32[]{:S(2)}) collective-permute-start(bf16[144,256]{1,0:T(8,128)(2,1)S(1)} %get-tuple-element.41), channel_id=1, source_target_pairs={{0,2},{1,3},{2,0},{3,1},{4,6},{5,7},{6,4},{7,5},{8,10},{9,11},{10,... | collective-permute-start | bytes 221192 | tf_op jit(solution)/shard_map/ppermute | solution.py:293
  130.0 20.2 %collective-permute-start.6 = (bf16[144,256]{1,0:T(8,128)(2,1)S(1)}, bf16[144,256]{1,0:T(8,128)(2,1)S(1)}, u32[]{:S(2)}, u32[]{:S(2)}) collective-permute-start(bf16[144,256]{1,0:T(8,128)(2,1)S(1)} %get-tuple-element.42), channel_id=1, source_target_pairs={{0,3},{1,2},{2,1},{3,0},{4,7},{5,6},{6,5},{7,4},{8,11},{9,10},{10,... | collective-permute-start | bytes 221192 | tf_op jit(solution)/shard_map/ppermute | solution.py:293
  131.4 3.4 %copy-start.1 = (f32[512,4096]{1,0:T(8,128)S(1)}, f32[512,4096]{1,0:T(8,128)}, u32[]{:S(2)}) copy-start(f32[512,4096]{1,0:T(8,128)} %copy-done) | copy-start | bytes 25165828
  136.9 25.1 %copy-start.5 = (f32[2,2,2,128,64]{3,4,2,1,0:T(8,128)S(1)}, f32[2,2,2,128,64]{3,4,2,1,0:T(8,128)}, u32[]{:S(2)}) copy-start(f32[2,2,2,128,64]{3,4,2,1,0:T(8,128)} %param.8) | copy-start | bytes 786436
  150.2 10.7 %collective-permute-start.19 = (f32[2,64,256]{2,1,0:T(8,128)S(1)}, f32[2,64,256]{2,1,0:T(8,128)S(1)}, u32[]{:S(2)}, u32[]{:S(2)}) collective-permute-start(f32[2,64,256]{2,1,0:T(8,128)S(1)} %get-tuple-element.57), channel_id=1, source_target_pairs={{0,1},{1,0},{2,3},{3,2},{4,5},{5,4},{6,7},{7,6},{8,9},{9,8},{10,11... | collective-permute-start | bytes 393224 | tf_op jit(solution)/shard_map/ppermute | solution.py:293
  150.2 11.6 %collective-permute-start.20 = (f32[2,64,256]{2,1,0:T(8,128)S(1)}, f32[2,64,256]{2,1,0:T(8,128)S(1)}, u32[]{:S(2)}, u32[]{:S(2)}) collective-permute-start(f32[2,64,256]{2,1,0:T(8,128)S(1)} %get-tuple-element.58), channel_id=1, source_target_pairs={{0,2},{1,3},{2,0},{3,1},{4,6},{5,7},{6,4},{7,5},{8,10},{9,11},{10,... | collective-permute-start | bytes 393224 | tf_op jit(solution)/shard_map/ppermute | solution.py:293
  152.3 9.5 %collective-permute-start.21 = (f32[2,64,256]{2,1,0:T(8,128)S(1)}, f32[2,64,256]{2,1,0:T(8,128)S(1)}, u32[]{:S(2)}, u32[]{:S(2)}) collective-permute-start(f32[2,64,256]{2,1,0:T(8,128)S(1)} %get-tuple-element.59), channel_id=1, source_target_pairs={{0,3},{1,2},{2,1},{3,0},{4,7},{5,6},{6,5},{7,4},{8,11},{9,10},{10,... | collective-permute-start | bytes 393224 | tf_op jit(solution)/shard_map/ppermute | solution.py:293
  156.4 9.3 %collective-permute-start.7 = (bf16[144,256]{1,0:T(8,128)(2,1)S(1)}, bf16[144,256]{1,0:T(8,128)(2,1)S(1)}, u32[]{:S(2)}, u32[]{:S(2)}) collective-permute-start(bf16[144,256]{1,0:T(8,128)(2,1)S(1)} %get-tuple-element.43.rest_0_), channel_id=1, source_target_pairs={{0,8},{8,0},{16,24},{24,16},{1,9},{9,1},{17,25},{25,17},{2,10},{10... | collective-permute-start | bytes 221192 | tf_op jit(solution)/shard_map/ppermute | solution.py:293
  161.9 4.9 %collective-permute-start.22 = (f32[2,64,128]{2,1,0:T(8,128)S(1)}, f32[2,64,128]{2,1,0:T(8,128)S(1)}, u32[]{:S(2)}, u32[]{:S(2)}) collective-permute-start(f32[2,64,128]{2,1,0:T(8,128)S(1)} %constant_dynamic-slice_fusion), channel_id=1, source_target_pairs={{0,4},{4,0},{1,5},{5,1},{2,6},{6,2},{3,7},{7,3},{8,12},{12,8},{9,1... | collective-permute-start | bytes 196616 | tf_op jit(solution)/shard_map/ppermute | solution.py:407
  162.1 20.7 %collective-permute-start.8 = (bf16[144,256]{1,0:T(8,128)(2,1)S(1)}, bf16[144,256]{1,0:T(8,128)(2,1)S(1)}, u32[]{:S(2)}, u32[]{:S(2)}) collective-permute-start(bf16[144,256]{1,0:T(8,128)(2,1)S(1)} %get-tuple-element.43.rest_0_), channel_id=1, source_target_pairs={{0,16},{8,24},{16,0},{24,8},{1,17},{9,25},{17,1},{25,9},{2,18},{10... | collective-permute-start | bytes 221192 | tf_op jit(solution)/shard_map/ppermute | solution.py:293
  163.3 19.6 %collective-permute-start.9 = (bf16[144,256]{1,0:T(8,128)(2,1)S(1)}, bf16[144,256]{1,0:T(8,128)(2,1)S(1)}, u32[]{:S(2)}, u32[]{:S(2)}) collective-permute-start(bf16[144,256]{1,0:T(8,128)(2,1)S(1)} %get-tuple-element.43.rest_0_), channel_id=1, source_target_pairs={{0,24},{8,16},{16,8},{24,0},{1,25},{9,17},{17,9},{25,1},{2,26},{10... | collective-permute-start | bytes 221192 | tf_op jit(solution)/shard_map/ppermute | solution.py:293
  165.1 8.3 %collective-permute-start.16 = (bf16[144,768]{1,0:T(8,128)(2,1)S(1)}, bf16[144,768]{1,0:T(8,128)(2,1)S(1)}, u32[]{:S(2)}, u32[]{:S(2)}) collective-permute-start(bf16[144,768]{1,0:T(8,128)(2,1)S(1)} %get-tuple-element.52.rest_0_), channel_id=1, source_target_pairs={{0,8},{8,0},{16,24},{24,16},{1,9},{9,1},{17,25},{25,17},{2,10},{10... | collective-permute-start | bytes 663560 | tf_op jit(solution)/shard_map/ppermute | solution.py:293
  165.7 9.3 %collective-permute-start.17 = (bf16[144,768]{1,0:T(8,128)(2,1)S(1)}, bf16[144,768]{1,0:T(8,128)(2,1)S(1)}, u32[]{:S(2)}, u32[]{:S(2)}) collective-permute-start(bf16[144,768]{1,0:T(8,128)(2,1)S(1)} %get-tuple-element.52.rest_0_), channel_id=1, source_target_pairs={{0,16},{8,24},{16,0},{24,8},{1,17},{9,25},{17,1},{25,9},{2,18},{10... | collective-permute-start | bytes 663560 | tf_op jit(solution)/shard_map/ppermute | solution.py:293
  166.8 12.1 %collective-permute-start.18 = (bf16[144,768]{1,0:T(8,128)(2,1)S(1)}, bf16[144,768]{1,0:T(8,128)(2,1)S(1)}, u32[]{:S(2)}, u32[]{:S(2)}) collective-permute-start(bf16[144,768]{1,0:T(8,128)(2,1)S(1)} %get-tuple-element.52.rest_0_), channel_id=1, source_target_pairs={{0,24},{8,16},{16,8},{24,0},{1,25},{9,17},{17,9},{25,1},{2,26},{10... | collective-permute-start | bytes 663560 | tf_op jit(solution)/shard_map/ppermute | solution.py:293
  173.4 10.9 %collective-permute-start.23 = (f32[2,64,128]{2,1,0:T(8,128)S(1)}, f32[2,64,128]{2,1,0:T(8,128)S(1)}, u32[]{:S(2)}, u32[]{:S(2)}) collective-permute-start(f32[2,64,128]{2,1,0:T(8,128)S(1)} %bitcast_subtract_fusion), channel_id=1, source_target_pairs={{0,8},{8,0},{16,24},{24,16},{1,9},{9,1},{17,25},{25,17},{2,10},{10... | collective-permute-start | bytes 196616 | tf_op jit(solution)/shard_map/ppermute | solution.py:293
  175.0 9.3 %collective-permute-start.24 = (f32[2,64,128]{2,1,0:T(8,128)S(1)}, f32[2,64,128]{2,1,0:T(8,128)S(1)}, u32[]{:S(2)}, u32[]{:S(2)}) collective-permute-start(f32[2,64,128]{2,1,0:T(8,128)S(1)} %bitcast_subtract_fusion), channel_id=1, source_target_pairs={{0,16},{8,24},{16,0},{24,8},{1,17},{9,25},{17,1},{25,9},{2,18},{10... | collective-permute-start | bytes 196616 | tf_op jit(solution)/shard_map/ppermute | solution.py:293
  178.9 5.3 %collective-permute-start.25 = (f32[2,64,128]{2,1,0:T(8,128)S(1)}, f32[2,64,128]{2,1,0:T(8,128)S(1)}, u32[]{:S(2)}, u32[]{:S(2)}) collective-permute-start(f32[2,64,128]{2,1,0:T(8,128)S(1)} %bitcast_subtract_fusion), channel_id=1, source_target_pairs={{0,24},{8,16},{16,8},{24,0},{1,25},{9,17},{17,9},{25,1},{2,26},{10... | collective-permute-start | bytes 196616 | tf_op jit(solution)/shard_map/ppermute | solution.py:293
  (3 other events, 4.6 us)
Sparse Core Ops, SparseCore 0:
  10.1 83.4 all-gather.6
  95.2 34.0 all-gather.4

commit v3 on v2

--- a/solution.py
+++ b/solution.py
@@ -160,8 +160,16 @@
     )(scalars, own, *received)
 
 
-def col_body(n_in, nodes, own_ref, u_ref, *rest):
-    ins, (shared_ref, out_ref) = rest[:n_in], rest[n_in:]
+def gathered(u_refs, all_ref, owner_ref, at):
+    for k, ref in enumerate(u_refs):
+        all_ref[owner_ref[at + k]] = ref[...]
+    blocks, nodes = all_ref.shape[:2]
+    return [jnp.concatenate([all_ref[k, n] for k in range(blocks)], axis=0) for n in range(nodes)]
+
+
+def col_body(nodes, n_col, at, owner_ref, own_ref, *rest):
+    u_refs, ins, (shared_ref, out_ref, all_ref) = rest[:n_col], rest[n_col:-3], rest[-3:]
+    u = gathered(u_refs, all_ref, owner_ref, at)
     z = own_ref[...]
     for ref in ins:
         z = z + decode(ref[...])
@@ -175,27 +183,29 @@
 
     for n in range(nodes):
         rows = slice(n * half, (n + 1) * half)
-        shared_ref[n] += dot_nt(hi[rows], u_ref[n]) + dot_nt(lo[rows], u_ref[n])
-
-
-def col_call(tile, nodes, own, received, u, first):
+        shared_ref[n] += dot_nt(hi[rows], u[n]) + dot_nt(lo[rows], u[n])
+
+
+def col_call(tile, nodes, scalars, at, own, received, u, first):
     part, width = own.shape
-    size = u.shape[1]
-    block = lambda rows: pl.BlockSpec((rows, tile), lambda j: (0, j))
-    shared = jax.ShapeDtypeStruct((nodes, part // nodes, size), F32)
+    block = lambda rows: pl.BlockSpec((rows, tile), lambda j, w: (0, j))
+    some = u[0].shape[1]
+    shared = jax.ShapeDtypeStruct((nodes, part // nodes, some * len(u)), F32)
     return pl.pallas_call(
-        functools.partial(col_body, len(received), nodes),
-        grid=(width // tile,),
-        in_specs=[
-            block(part),
-            pl.BlockSpec((nodes, size, tile), lambda j: (0, 0, first // tile + j)),
-        ]
-        + [block(part + PAD)] * len(received),
-        out_specs=[pl.BlockSpec(shared.shape, lambda j: (0, 0, 0)), block(part + PAD)],
+        functools.partial(col_body, nodes, len(u), at),
+        grid_spec=pltpu.PrefetchScalarGridSpec(
+            num_scalar_prefetch=1,
+            grid=(width // tile,),
+            in_specs=[block(part)]
+            + [pl.BlockSpec((nodes, some, tile), lambda j, w: (0, 0, first // tile + j))] * len(u)
+            + [block(part + PAD)] * len(received),
+            out_specs=[pl.BlockSpec(shared.shape, lambda j, w: (0, 0, 0)), block(part + PAD)],
+            scratch_shapes=[pltpu.VMEM((len(u), nodes, some, tile), BF16)],
+        ),
         out_shape=[shared, jax.ShapeDtypeStruct((part + PAD, width), BF16)],
         compiler_params=pltpu.CompilerParams(vmem_limit_bytes=16 << 20),
         name="col_sum",
-    )(own, u, *received)
+    )(scalars, own, *u, *received)
 
 
 def place_body(n_in, at, at_ref, *rest):
@@ -235,8 +245,9 @@
     return hi, (x - hi.astype(F32)).astype(BF16)
 
 
-def project_body(halves, nodes, per_col, n_col, at, where_ref, z_ref, u_ref, *rest):
-    outs, acc_ref = rest[:n_col], rest[-1]
+def project_body(halves, nodes, per_col, n_col, at, owners, where_ref, z_ref, *rest):
+    u_refs, outs, (acc_ref, all_ref) = rest[:n_col], rest[n_col:-2], rest[-2:]
+    u = gathered(u_refs, all_ref, where_ref, owners)
     half = z_ref.shape[0] // (halves * nodes)
     step = pl.program_id(0)
 
@@ -247,7 +258,7 @@
     for n in range(nodes):
         rows = [split(z_ref[pl.ds((h * nodes + n) * half, half)]) for h in range(halves)]
         both = jnp.concatenate([x[0] for x in rows] + [x[1] for x in rows], axis=0)
-        result = dot_nt(both, u_ref[n])
+        result = dot_nt(both, u[n])
         for h in range(halves):
             low = result[(halves + h) * half : (halves + h + 1) * half]
             acc_ref[h, n] += result[h * half : (h + 1) * half] + low
@@ -259,26 +270,30 @@
             out[...] = acc_ref[where_ref[at + 2 * k], :, pl.ds(first, per_col), :]
 
 
-def project_call(halves, nodes, per_col, n_col, tile, scalars, at, z, u):
+def project_call(halves, nodes, per_col, n_col, tile, scalars, at, owners, z, u):
     flat, rows = z.shape
-    size = u.shape[1]
+    some = u[0].shape[1]
+    size = some * n_col
     out = jax.ShapeDtypeStruct((nodes, per_col, size), F32)
     return pl.pallas_call(
-        functools.partial(project_body, halves, nodes, per_col, n_col, at),
+        functools.partial(project_body, halves, nodes, per_col, n_col, at, owners),
         grid_spec=pltpu.PrefetchScalarGridSpec(
             num_scalar_prefetch=1,
             grid=(rows // tile,),
             in_specs=[
                 pl.BlockSpec((flat, tile), lambda j, w: (0, j)),
-                pl.BlockSpec((nodes, size, tile), lambda j, w: (0, 0, j)),
+            ]
+            + [pl.BlockSpec((nodes, some, tile), lambda j, w: (0, 0, j))] * n_col,
+            out_specs=[pl.BlockSpec(out.shape, lambda j, w: (0, 0, 0))] * n_col,
+            scratch_shapes=[
+                pltpu.VMEM((halves, nodes, flat // (halves * nodes), size), F32),
+                pltpu.VMEM((n_col, nodes, some, tile), BF16),
             ],
-            out_specs=[pl.BlockSpec(out.shape, lambda j, w: (0, 0, 0))] * n_col,
-            scratch_shapes=[pltpu.VMEM((halves, nodes, flat // (halves * nodes), size), F32)],
         ),
         out_shape=[out] * n_col,
         compiler_params=pltpu.CompilerParams(vmem_limit_bytes=24 << 20),
         name="project",
-    )(scalars, z, u)
+    )(scalars, z, *u)
 
 
 def peer(i, k, n):
@@ -303,7 +318,7 @@
     quarter = rows // n_pole
     if quarter % 1024 == 0 and n_pole == 4:
         widths = [quarter * 3 // 4, quarter // 4]
-        calls = [[(0, 3)], [(0, 2), (0, 1)], [(1, 3), (0, 0)], [(1, 2), (1, 1)], [(1, 0)]]
+        calls = [[(0, 3), (0, 2)], [(0, 1), (0, 0)], [(1, 3), (1, 2), (1, 1)], [(1, 0)]]
         return widths, calls
     return [quarter], [[(0, k)] for k in reversed(range(n_pole))]
 
@@ -329,6 +344,13 @@
     top = jnp.max(jnp.abs(pole_weights)) * poles
     scale = jnp.where(top > 0, 2.0**19 / jnp.maximum(top, 1e-30), 1.0)
     weights = jnp.concatenate([(pole_weights * scale).reshape(-1), (1.0 / scale).reshape(1)])
+
+    weight_real = pole_weights[:, 0].reshape(-1, 1, 1, 1)
+    weight_imag = pole_weights[:, 1].reshape(-1, 1, 1, 1)
+    weighted_diag = jnp.sum(
+        weight_real * diag_inverse[:, :, 1] + weight_imag * diag_inverse[:, :, 0], axis=0
+    ).transpose(0, 2, 1)
+    weights, weighted_diag = lax.optimization_barrier((weights, weighted_diag))
 
     quarter = rows // n_pole
     widths, calls = plan_of(rows, n_pole)
@@ -352,12 +374,15 @@
         per_half = half // per_col
         h = target // per_half
         numbers += [h ^ r if halves == 2 else h, target % per_half * per_col]
+    owners = len(numbers)
+    numbers += [(c + n_col - k) % n_col for k in range(n_col)]
     scalars = jnp.stack([jnp.asarray(x, jnp.int32) for x in numbers])
 
-    upper_imag = upper_factor[:, 1]
-    upper_imag = lax.all_gather(upper_imag, "col", axis=1, tiled=True)
-    upper_real = lax.dynamic_slice_in_dim(upper_factor[:, 0], p * quarter, quarter, 2)
-    upper_real = lax.all_gather(upper_real, "col", axis=1, tiled=True)
+    mine = lax.dynamic_slice_in_dim(upper_factor[:, 0], p * quarter, quarter, 2)
+    upper = [jnp.concatenate([upper_factor[:, 1], mine], axis=2)]
+    for _ in range(1, n_col):
+        ring = [(i, (i + 1) % n_col) for i in range(n_col)]
+        upper.append(lax.ppermute(upper[-1], "col", ring))
 
     real = out = None
     shared = []
@@ -382,25 +407,20 @@
             received = []
             for k, x in enumerate(parts):
                 received.append(send(x, "col", k + 1, n_col))
-            projected, payload = col_call(tile, nodes, own, received, upper_real, firsts[g])
+            projected, payload = col_call(
+                tile, nodes, scalars, owners, own, received, upper, rows + firsts[g]
+            )
             shared.append(projected)
             payloads = [payload]
             for k in range(1, n_pole):
                 payloads.append(send(payload, "pole", k, n_pole))
             out = place_call(rows, scalars, puts[g], payloads, out)
 
-    parts = project_call(
-        halves, nodes, per_col, n_col, step, scalars, where, real, upper_imag
-    )
+    parts = project_call(halves, nodes, per_col, n_col, step, scalars, where, owners, real, upper)
     shared.append(parts[0])
     for k in range(1, n_col):
         shared.append(send(parts[k], "col", k, n_col))
     shared = sum(shared[1:], shared[0])
-    weight_real = pole_weights[:, 0].reshape(-1, 1, 1, 1)
-    weight_imag = pole_weights[:, 1].reshape(-1, 1, 1, 1)
-    weighted_diag = jnp.sum(
-        weight_real * diag_inverse[:, :, 1] + weight_imag * diag_inverse[:, :, 0], axis=0
-    ).transpose(0, 2, 1)
     if n_row == 2:
         keep = lax.dynamic_slice_in_dim(shared, r * s_row, s_row, 2)
         give = lax.dynamic_slice_in_dim(shared, (1 - r) * s_row, s_row, 2)

time: 192 us -> 245 us (1.28)
  waiting for transfers between devices: 21.6 us -> 89.6 us
  between operations: 15.5 us -> 1.69 us
  local copies, waits for them, and re-layouts: 15.1 us -> 11.8 us
  starting transfers between devices: 37.3 us -> 34.7 us
  other arithmetic: 6.15 us -> 8.68 us
    ppermute x0 -> x3, waiting for transfers between devices: none -> 57.5 us  [per_device(): upper.append(lax.ppermute(upper[-1], 'col', ring))]
    ppermute x24, waiting for transfers between devices: 20.3 us -> 32.1 us  [send(): return lax.ppermute(x, axis, [(i, peer(i, k, n)) for i in range(n)])]
    ppermute x24, starting transfers between devices: 36.6 us -> 31.6 us  [send(): return lax.ppermute(x, axis, [(i, peer(i, k, n)) for i in range(n)])]
    unnamed x16 -> x34, local copies, waits for them, and re-layouts: 14.7 us -> 9.67 us
    pallas_call x5 -> x4, Pallas kernels: 80.9 us -> 76.9 us  [main_call(): pl.pallas_call(functools.partial(main_body, outs, steps, halves, nodes),...]
    pallas_call x2, Pallas kernels: 2.09 us -> 5.33 us  [col_call(): pl.pallas_call(functools.partial(col_body, nodes, len(u), at), grid_spec=...]
    ppermute x0 -> x3, starting transfers between devices: none -> 3.11 us  [per_device(): upper.append(lax.ppermute(upper[-1], 'col', ring))]
  transfers between devices with their start and end apart: 28 -> 29, of which waited for: 8 -> 9; matrix products, arithmetic and copies ran while one was open for 3% -> 3% of each run, Pallas kernels for 50% -> 40%
where the time goes in v3:
time: 245 us
  Pallas kernels  98.2 us (40%)
  waiting for transfers between devices  89.6 us (37%)
  starting transfers between devices  34.7 us (14%)
  local copies, waits for them, and re-layouts  11.8 us (5%)
  other arithmetic  8.68 us (4%)
    pallas_call x4, Pallas kernels, main_call(): pl.pallas_call(functools.partial(main_body, outs, steps, halves, nodes),...  76.9 us
    ppermute x3, waiting for transfers between devices, per_device(): upper.append(lax.ppermute(upper[-1], 'col', ring))  57.5 us
    ppermute x24, waiting for transfers between devices, send(): return lax.ppermute(x, axis, [(i, peer(i, k, n)) for i in range(n)])  32.1 us
    ppermute x24, starting transfers between devices, send(): return lax.ppermute(x, axis, [(i, peer(i, k, n)) for i in range(n)])  31.6 us
    unnamed x34, local copies, waits for them, and re-layouts  9.67 us
    pallas_call x1, Pallas kernels, project_call(): pl.pallas_call(functools.partial(project_body, halves, nodes, per_col, n_...  6.53 us
    pallas_call x2, Pallas kernels, pole_call(): pl.pallas_call(functools.partial(pole_body, nodes, per_col, len(received)...  5.83 us
    pallas_call x2, Pallas kernels, col_call(): pl.pallas_call(functools.partial(col_body, nodes, len(u), at), grid_spec=...  5.33 us
  transfers between devices with their start and end apart: 29, of which 9 were waited for; matrix products, arithmetic and copies ran while one was open for 3% of the time, Pallas kernels for 40%

profile of v3, /device:TPU:0, one launch (start us, length us, event | category | flops | bytes accessed | tf_op | source)
XLA Modules:
  0.0 244.7 jit_solution(602196389006656283)
XLA Ops:
  0.6 1.8 slice_bitcast_fusion
  2.6 3.1 %collective-permute-start.4 = (bf16[2,64,5120]{2,1,0:T(8,128)(2,1)S(1)}, bf16[2,64,5120]{2,1,0:T(8,128)(2,1)S(1)}, u32[]{:S(2)}, u32[]{:S(2)}) collective-permute-start(bf16[2,64,5120]{2,1,0:T(8,128)(2,1)S(1)} %pad_maximum_fusion.1.rest_0_), channel_id=1, source_target_pairs={{0,1},{1,2},{2,3},{3,0},{4,5},{5,6},{6,7},{7,4},{8,9},{9,10},{10,1... | collective-permute-start | bytes 3932168 | tf_op jit(solution)/shard_map/ppermute | solution.py:385
  5.7 30.8 %collective-permute-done.4.rest_1_ = bf16[2,64,5120]{2,1,0:T(8,128)(2,1)S(1)} collective-permute-done((bf16[2,64,5120]{2,1,0:T(8,128)(2,1)S(1)}, bf16[2,64,5120]{2,1,0:T(8,128)(2,1)S(1)}, u32[]{:S(2)}, u32[]{:S(2)}) %collective-permute-start.4) | collective-permute-done | bytes 1310752 | tf_op jit(solution)/shard_map/ppermute | solution.py:385
  39.0 2.6 %pad_maximum_fusion = bf16[2,2,2,128,2048]{4,3,2,1,0:T(8,128)(2,1)S(1)} fusion(bf16[1,2,2,128,2048]{4,3,2,1,0:T(8,128)(2,1)} %bitcast.41, bf16[1,2,2,128,2048]{4,3,2,1,0:T(8,128)(2,1)} %bitcast.40), kind=kLoop, calls=%fused_computation | loop fusion | flops 2097152 | bytes 8388608 | tf_op jit(solution)/shard_map/stack | solution.py:337
  41.6 26.7 %collective-permute-done.5.rest_2_ = bf16[2,64,5120]{2,1,0:T(8,128)(2,1)} collective-permute-done((bf16[2,64,5120]{2,1,0:T(8,128)(2,1)S(1)}, bf16[2,64,5120]{2,1,0:T(8,128)(2,1)}, u32[]{:S(2)}, u32[]{:S(2)}) %collective-permute-start.5) | collective-permute-done | bytes 1310752 | tf_op jit(solution)/shard_map/ppermute | solution.py:385
  68.3 2.0 bitcast_convert_fusion.rest_1_
  70.3 27.5 %products.4 = (f32[512,4096]{1,0:T(8,128)S(1)}, bf16[528,768]{1,0:T(8,128)(2,1)S(1)}, bf16[528,768]{1,0:T(8,128)(2,1)S(1)}) custom-call(s32[36]{0:T(128)S(1)} %stack.156.base_ref.where_ref.owner_ref.at_ref, f32[5]{0:T(128)S(1)} %pad_maximum_fusion.2.w_ref, bf16[2,2,4096,2048]{3,2,1,0:T(8,128)(2,1)} %g_ref.7, bf16[1024,2048]{1,0:T(8,128)(2,1)S(1)} %bitcast.65, ...), custom_call_target="tpu_custom_call" | custom-call | tf_op jit(solution)/shard_map/products/pallas_call | solution.py:116
  97.8 27.6 %products.5 = (f32[512,4096]{1,0:T(8,128)S(1)}, bf16[528,768]{1,0:T(8,128)(2,1)S(1)}, f32[512,768]{1,0:T(8,128)S(1)}) custom-call(s32[36]{0:T(128)S(1)} %stack.156.base_ref.where_ref.owner_ref.at_ref, f32[5]{0:T(128)S(1)} %pad_maximum_fusion.2.w_ref, bf16[2,2,4096,2048]{3,2,1,0:T(8,128)(2,1)} %g_ref.7, ...), custom_call_target="tpu_custom_call", output_to_operand_aliasing={{0}: (5, {})} | custom-call | tf_op jit(solution)/shard_map/products/pallas_call | solution.py:116
  126.8 1.5 collective-permute-start.14
  129.0 15.2 %products.6 = (f32[512,4096]{1,0:T(8,128)S(1)}, bf16[528,256]{1,0:T(8,128)(2,1)S(1)}, bf16[528,256]{1,0:T(8,128)(2,1)S(1)}, bf16[528,256]{1,0:T(8,128)(2,1)S(1)}) custom-call(s32[36]{0:T(128)S(1)} %stack.156.base_ref.where_ref.owner_ref.at_ref, f32[5]{0:T(128)S(1)} %pad_maximum_fusion.2.w_ref, ...), custom_call_target="tpu_custom_call", output_to_operand_aliasing={{0}: (5, {})} | custom-call | tf_op jit(solution)/shard_map/products/pallas_call | solution.py:116
  147.8 14.2 %collective-permute-done.14.rest_1_ = bf16[528,768]{1,0:T(8,128)(2,1)S(1)} collective-permute-done((bf16[528,768]{1,0:T(8,128)(2,1)S(1)}, bf16[528,768]{1,0:T(8,128)(2,1)S(1)}, u32[]{:S(2)}, u32[]{:S(2)}) %collective-permute-start.14) | collective-permute-done | bytes 811040 | tf_op jit(solution)/shard_map/ppermute | solution.py:308
  162.0 1.6 collective-permute-start.3
  164.6 4.3 %pole_sum.3 = (f32[128,768]{1,0:T(8,128)S(1)}, bf16[144,768]{1,0:T(8,128)(2,1)S(1)}, bf16[144,768]{1,0:T(8,128)(2,1)}, bf16[144,768]{1,0:T(8,128)(2,1)}) custom-call(s32[36]{0:T(128)S(1)} %stack.156.base_ref.where_ref.owner_ref.at_ref, f32[512,768]{1,0:T(8,128)S(1)} %get-tuple-element.45.own_ref, bf16[528,768]{1,0:T(8,128)(2,1)S(1)} %collective-permute-done.13.rest_0_, ...), custom_call_target="tpu_custom_call" | custom-call | tf_op jit(solution)/shard_map/pole_sum/pallas_call | solution.py:147
  169.0 6.6 %products.7 = (f32[512,4096]{1,0:T(8,128)S(1)}, f32[512,256]{1,0:T(8,128)S(1)}) custom-call(s32[36]{0:T(128)S(1)} %stack.156.base_ref.where_ref.owner_ref.at_ref, f32[5]{0:T(128)S(1)} %pad_maximum_fusion.2.w_ref, bf16[2,2,4096,2048]{3,2,1,0:T(8,128)(2,1)} %g_ref.7, bf16[1024,2048]{1,0:T(8,128)(2,1)S(1)} %bitcast.68, ...), custom_call_target="tpu_custom_call", output_to_operand_aliasing={{0}: (5, {})} | custom-call | tf_op jit(solution)/shard_map/products/pallas_call | solution.py:116
  175.6 1.5 pole_sum.2
  177.7 2.0 collective-permute-start.7
  179.8 2.4 collective-permute-start.17
  182.1 1.5 collective-permute-start.18
  184.9 2.2 collective-permute-start.8
  187.9 6.5 %project.1 = (f32[2,64,256]{2,1,0:T(8,128)S(1)}, f32[2,64,256]{2,1,0:T(8,128)}, f32[2,64,256]{2,1,0:T(8,128)}, f32[2,64,256]{2,1,0:T(8,128)}) custom-call(s32[36]{0:T(128)S(1)} %stack.156.base_ref.where_ref.owner_ref.at_ref, f32[512,4096]{1,0:T(8,128)S(1)} %get-tuple-element.57.z_ref, bf16[2,64,5120]{2,1,0:T(8,128)(2,1)S(1)} %pad_maximum_fusion.1.rest_0_, ...), custom_call_target="tpu_custom_call" | custom-call | tf_op jit(solution)/shard_map/project/pallas_call | solution.py:278
  195.1 6.9 %collective-permute-done.8.rest_5_ = bf16[144,256]{1,0:T(8,128)(2,1)S(1)} collective-permute-done((bf16[144,256]{1,0:T(8,128)(2,1)S(1)}, bf16[144,256]{1,0:T(8,128)(2,1)S(1)}, u32[]{:S(2)}, u32[]{:S(2)}) %collective-permute-start.8) | collective-permute-done | bytes 73760 | tf_op jit(solution)/shard_map/ppermute | solution.py:308
  203.6 3.4 %collective-permute-start.23 = (f32[2,64,256]{2,1,0:T(8,128)}, f32[2,64,256]{2,1,0:T(8,128)}, u32[]{:S(2)}, u32[]{:S(2)}) collective-permute-start(f32[2,64,256]{2,1,0:T(8,128)} %get-tuple-element.60), channel_id=1, source_target_pairs={{0,2},{1,3},{2,0},{3,1},{4,6},{5,7},{6,4},{7,5},{8,10},{9,11},{10,... | collective-permute-start | bytes 393224 | tf_op jit(solution)/shard_map/ppermute | solution.py:308
  212.5 1.7 col_sum.2
  214.9 1.5 collective-permute-start.10
  217.4 3.6 %col_sum.3 = (f32[2,64,256]{2,1,0:T(8,128)S(1)}, bf16[144,768]{1,0:T(8,128)(2,1)S(1)}) custom-call(s32[36]{0:T(128)S(1)} %stack.156.base_ref.where_ref.owner_ref.at_ref, f32[128,768]{1,0:T(8,128)S(1)} %get-tuple-element.49.own_ref, bf16[2,64,5120]{2,1,0:T(8,128)(2,1)S(1)} %pad_maximum_fusion.1.rest_0_, ...), custom_call_target="tpu_custom_call" | custom-call | tf_op jit(solution)/shard_map/col_sum/pallas_call | solution.py:194
  224.0 1.7 collective-permute-start.21
  226.3 1.5 collective-permute-start.12
  228.6 1.9 collective-permute-done.19.rest_1_
  231.1 6.3 %collective-permute-done.20.rest_2_ = bf16[144,768]{1,0:T(8,128)(2,1)S(1)} collective-permute-done((bf16[144,768]{1,0:T(8,128)(2,1)S(1)}, bf16[144,768]{1,0:T(8,128)(2,1)S(1)}, u32[]{:S(2)}, u32[]{:S(2)}) %collective-permute-start.20) | collective-permute-done | bytes 221216 | tf_op jit(solution)/shard_map/ppermute | solution.py:308
  238.7 1.7 collective-permute-start.28
  240.4 1.8 place.2.rest_4_
  242.2 1.8 place.3
  (87 shorter events, 27.5 us)
Async XLA Ops:
  2.4 34.1 %copy-start.16 = (f32[2,2]{1,0:T(2,128)S(1)}, f32[2,2]{1,0:T(2,128)}, u32[]{:S(2)}) copy-start(f32[2,2]{1,0:T(2,128)} %param.9) | copy-start | bytes 52
  2.4 35.8 %copy-start.15 = (f32[2,2,2,128,64]{3,4,2,1,0:T(8,128)S(1)}, f32[2,2,2,128,64]{3,4,2,1,0:T(8,128)}, u32[]{:S(2)}) copy-start(f32[2,2,2,128,64]{3,4,2,1,0:T(8,128)} %param.8) | copy-start | bytes 786436
  2.6 33.9 %collective-permute-start.4 = (bf16[2,64,5120]{2,1,0:T(8,128)(2,1)S(1)}, bf16[2,64,5120]{2,1,0:T(8,128)(2,1)S(1)}, u32[]{:S(2)}, u32[]{:S(2)}) collective-permute-start(bf16[2,64,5120]{2,1,0:T(8,128)(2,1)S(1)} %pad_maximum_fusion.1.rest_0_), channel_id=1, source_target_pairs={{0,1},{1,2},{2,3},{3,0},{4,5},{5,6},{6,7},{7,4},{8,9},{9,10},{10,1... | collective-permute-start | bytes 3932168 | tf_op jit(solution)/shard_map/ppermute | solution.py:385
  5.7 33.3 %collective-permute-start = (bf16[2,2,128,2048]{3,2,1,0:T(8,128)(2,1)}, bf16[2,2,128,2048]{3,2,1,0:T(8,128)(2,1)}, u32[]{:S(2)}, u32[]{:S(2)}) collective-permute-start(bf16[2,2,128,2048]{3,2,1,0:T(8,128)(2,1)} %param.6), channel_id=1, source_target_pairs={{0,4},{4,0},{1,5},{5,1},{2,6},{6,2},{3,7},{7,3},{8,12},{12,8},{9,1... | collective-permute-start | bytes 6291464 | tf_op jit(solution)/shard_map/ppermute | solution.py:336
  36.5 31.8 %collective-permute-start.5 = (bf16[2,64,5120]{2,1,0:T(8,128)(2,1)S(1)}, bf16[2,64,5120]{2,1,0:T(8,128)(2,1)}, u32[]{:S(2)}, u32[]{:S(2)}) collective-permute-start(bf16[2,64,5120]{2,1,0:T(8,128)(2,1)S(1)} %collective-permute-done.4.rest_1_), channel_id=1, source_target_pairs={{0,1},{1,2},{2,3},{3,0},{4,5},{5,6},{6,7},{7,4},{8,9},{9,10},{10,1... | collective-permute-start | bytes 3932168 | tf_op jit(solution)/shard_map/ppermute | solution.py:385
  68.3 118.8 %collective-permute-start.6 = (bf16[2,64,5120]{2,1,0:T(8,128)(2,1)}, bf16[2,64,5120]{2,1,0:T(8,128)(2,1)S(1)}, u32[]{:S(2)}, u32[]{:S(2)}) collective-permute-start(bf16[2,64,5120]{2,1,0:T(8,128)(2,1)} %collective-permute-done.5.rest_2_), channel_id=1, source_target_pairs={{0,1},{1,2},{2,3},{3,0},{4,5},{5,6},{6,7},{7,4},{8,9},{9,10},{10,1... | collective-permute-start | bytes 3932168 | tf_op jit(solution)/shard_map/ppermute | solution.py:385
  125.5 21.0 %collective-permute-start.13 = (bf16[528,768]{1,0:T(8,128)(2,1)S(1)}, bf16[528,768]{1,0:T(8,128)(2,1)S(1)}, u32[]{:S(2)}, u32[]{:S(2)}) collective-permute-start(bf16[528,768]{1,0:T(8,128)(2,1)S(1)} %get-tuple-element.46), channel_id=1, source_target_pairs={{0,8},{8,0},{16,24},{24,16},{1,9},{9,1},{17,25},{25,17},{2,10},{10... | collective-permute-start | bytes 2433032 | tf_op jit(solution)/shard_map/ppermute | solution.py:308
  126.8 35.2 %collective-permute-start.14 = (bf16[528,768]{1,0:T(8,128)(2,1)S(1)}, bf16[528,768]{1,0:T(8,128)(2,1)S(1)}, u32[]{:S(2)}, u32[]{:S(2)}) collective-permute-start(bf16[528,768]{1,0:T(8,128)(2,1)S(1)} %get-tuple-element.47), channel_id=1, source_target_pairs={{0,16},{8,24},{16,0},{24,8},{1,17},{9,25},{17,1},{25,9},{2,18},{10... | collective-permute-start | bytes 2433032 | tf_op jit(solution)/shard_map/ppermute | solution.py:308
  128.3 36.3 %collective-permute-start.15 = (bf16[528,768]{1,0:T(8,128)(2,1)S(1)}, bf16[528,768]{1,0:T(8,128)(2,1)S(1)}, u32[]{:S(2)}, u32[]{:S(2)}) collective-permute-start(bf16[528,768]{1,0:T(8,128)(2,1)S(1)} %get-tuple-element.48), channel_id=1, source_target_pairs={{0,24},{8,16},{16,8},{24,0},{1,25},{9,17},{17,9},{25,1},{2,26},{10... | collective-permute-start | bytes 2433032 | tf_op jit(solution)/shard_map/ppermute | solution.py:308
  144.2 31.4 %collective-permute-start.1 = (bf16[528,256]{1,0:T(8,128)(2,1)S(1)}, bf16[528,256]{1,0:T(8,128)(2,1)S(1)}, u32[]{:S(2)}, u32[]{:S(2)}) collective-permute-start(bf16[528,256]{1,0:T(8,128)(2,1)S(1)} %get-tuple-element.37), channel_id=1, source_target_pairs={{0,8},{8,0},{16,24},{24,16},{1,9},{9,1},{17,25},{25,17},{2,10},{10... | collective-permute-start | bytes 811016 | tf_op jit(solution)/shard_map/ppermute | solution.py:308
  146.5 29.1 %collective-permute-start.2 = (bf16[528,256]{1,0:T(8,128)(2,1)S(1)}, bf16[528,256]{1,0:T(8,128)(2,1)S(1)}, u32[]{:S(2)}, u32[]{:S(2)}) collective-permute-start(bf16[528,256]{1,0:T(8,128)(2,1)S(1)} %get-tuple-element.38), channel_id=1, source_target_pairs={{0,16},{8,24},{16,0},{24,8},{1,17},{9,25},{17,1},{25,9},{2,18},{10... | collective-permute-start | bytes 811016 | tf_op jit(solution)/shard_map/ppermute | solution.py:308
  162.0 13.6 %collective-permute-start.3 = (bf16[528,256]{1,0:T(8,128)(2,1)S(1)}, bf16[528,256]{1,0:T(8,128)(2,1)S(1)}, u32[]{:S(2)}, u32[]{:S(2)}) collective-permute-start(bf16[528,256]{1,0:T(8,128)(2,1)S(1)} %get-tuple-element.39), channel_id=1, source_target_pairs={{0,24},{8,16},{16,8},{24,0},{1,25},{9,17},{17,9},{25,1},{2,26},{10... | collective-permute-start | bytes 811016 | tf_op jit(solution)/shard_map/ppermute | solution.py:308
  169.0 38.1 %collective-permute-start.16 = (bf16[144,768]{1,0:T(8,128)(2,1)S(1)}, bf16[144,768]{1,0:T(8,128)(2,1)S(1)}, u32[]{:S(2)}, u32[]{:S(2)}) collective-permute-start(bf16[144,768]{1,0:T(8,128)(2,1)S(1)} %get-tuple-element.50), channel_id=1, source_target_pairs={{0,1},{1,0},{2,3},{3,2},{4,5},{5,4},{6,7},{7,6},{8,9},{9,8},{10,11... | collective-permute-start | bytes 663560 | tf_op jit(solution)/shard_map/ppermute | solution.py:308
  177.7 6.5 %collective-permute-start.7 = (bf16[144,256]{1,0:T(8,128)(2,1)S(1)}, bf16[144,256]{1,0:T(8,128)(2,1)S(1)}, u32[]{:S(2)}, u32[]{:S(2)}) collective-permute-start(bf16[144,256]{1,0:T(8,128)(2,1)S(1)} %get-tuple-element.41), channel_id=1, source_target_pairs={{0,1},{1,0},{2,3},{3,2},{4,5},{5,4},{6,7},{7,6},{8,9},{9,8},{10,11... | collective-permute-start | bytes 221192 | tf_op jit(solution)/shard_map/ppermute | solution.py:308
  179.8 34.5 %collective-permute-start.17 = (bf16[144,768]{1,0:T(8,128)(2,1)}, bf16[144,768]{1,0:T(8,128)(2,1)S(1)}, u32[]{:S(2)}, u32[]{:S(2)}) collective-permute-start(bf16[144,768]{1,0:T(8,128)(2,1)} %get-tuple-element.51), channel_id=1, source_target_pairs={{0,2},{1,3},{2,0},{3,1},{4,6},{5,7},{6,4},{7,5},{8,10},{9,11},{10,... | collective-permute-start | bytes 663560 | tf_op jit(solution)/shard_map/ppermute | solution.py:308
  182.1 34.3 %collective-permute-start.18 = (bf16[144,768]{1,0:T(8,128)(2,1)}, bf16[144,768]{1,0:T(8,128)(2,1)}, u32[]{:S(2)}, u32[]{:S(2)}) collective-permute-start(bf16[144,768]{1,0:T(8,128)(2,1)} %get-tuple-element.52), channel_id=1, source_target_pairs={{0,3},{1,2},{2,1},{3,0},{4,7},{5,6},{6,5},{7,4},{8,11},{9,10},{10,... | collective-permute-start | bytes 663560 | tf_op jit(solution)/shard_map/ppermute | solution.py:308
  184.9 17.1 %collective-permute-start.8 = (bf16[144,256]{1,0:T(8,128)(2,1)S(1)}, bf16[144,256]{1,0:T(8,128)(2,1)S(1)}, u32[]{:S(2)}, u32[]{:S(2)}) collective-permute-start(bf16[144,256]{1,0:T(8,128)(2,1)S(1)} %get-tuple-element.42), channel_id=1, source_target_pairs={{0,2},{1,3},{2,0},{3,1},{4,6},{5,7},{6,4},{7,5},{8,10},{9,11},{10,... | collective-permute-start | bytes 221192 | tf_op jit(solution)/shard_map/ppermute | solution.py:308
  187.1 7.3 %copy-start = (bf16[2,64,5120]{2,1,0:T(8,128)(2,1)}, bf16[2,64,5120]{2,1,0:T(8,128)(2,1)S(1)}, u32[]{:S(2)}) copy-start(bf16[2,64,5120]{2,1,0:T(8,128)(2,1)S(1)} %collective-permute-done.6.rest_3_) | copy-start | bytes 3932164
  187.1 15.9 %collective-permute-start.9 = (bf16[144,256]{1,0:T(8,128)(2,1)S(1)}, bf16[144,256]{1,0:T(8,128)(2,1)S(1)}, u32[]{:S(2)}, u32[]{:S(2)}) collective-permute-start(bf16[144,256]{1,0:T(8,128)(2,1)S(1)} %get-tuple-element.43), channel_id=1, source_target_pairs={{0,3},{1,2},{2,1},{3,0},{4,7},{5,6},{6,5},{7,4},{8,11},{9,10},{10,... | collective-permute-start | bytes 221192 | tf_op jit(solution)/shard_map/ppermute | solution.py:308
  202.6 18.4 %collective-permute-start.22 = (f32[2,64,256]{2,1,0:T(8,128)}, f32[2,64,256]{2,1,0:T(8,128)}, u32[]{:S(2)}, u32[]{:S(2)}) collective-permute-start(f32[2,64,256]{2,1,0:T(8,128)} %get-tuple-element.59), channel_id=1, source_target_pairs={{0,1},{1,0},{2,3},{3,2},{4,5},{5,4},{6,7},{7,6},{8,9},{9,8},{10,11... | collective-permute-start | bytes 393224 | tf_op jit(solution)/shard_map/ppermute | solution.py:308
  203.6 17.4 %collective-permute-start.23 = (f32[2,64,256]{2,1,0:T(8,128)}, f32[2,64,256]{2,1,0:T(8,128)}, u32[]{:S(2)}, u32[]{:S(2)}) collective-permute-start(f32[2,64,256]{2,1,0:T(8,128)} %get-tuple-element.60), channel_id=1, source_target_pairs={{0,2},{1,3},{2,0},{3,1},{4,6},{5,7},{6,4},{7,5},{8,10},{9,11},{10,... | collective-permute-start | bytes 393224 | tf_op jit(solution)/shard_map/ppermute | solution.py:308
  207.0 14.0 %collective-permute-start.24 = (f32[2,64,256]{2,1,0:T(8,128)}, f32[2,64,256]{2,1,0:T(8,128)}, u32[]{:S(2)}, u32[]{:S(2)}) collective-permute-start(f32[2,64,256]{2,1,0:T(8,128)} %get-tuple-element.61), channel_id=1, source_target_pairs={{0,3},{1,2},{2,1},{3,0},{4,7},{5,6},{6,5},{7,4},{8,11},{9,10},{10,... | collective-permute-start | bytes 393224 | tf_op jit(solution)/shard_map/ppermute | solution.py:308
  214.9 10.8 %collective-permute-start.10 = (bf16[144,256]{1,0:T(8,128)(2,1)S(1)}, bf16[144,256]{1,0:T(8,128)(2,1)}, u32[]{:S(2)}, u32[]{:S(2)}) collective-permute-start(bf16[144,256]{1,0:T(8,128)(2,1)S(1)} %get-tuple-element.44.rest_0_), channel_id=1, source_target_pairs={{0,8},{8,0},{16,24},{24,16},{1,9},{9,1},{17,25},{25,17},{2,10},{10... | collective-permute-start | bytes 221192 | tf_op jit(solution)/shard_map/ppermute | solution.py:308
  222.1 4.1 %collective-permute-start.25 = (f32[2,64,128]{2,1,0:T(8,128)S(1)}, f32[2,64,128]{2,1,0:T(8,128)S(1)}, u32[]{:S(2)}, u32[]{:S(2)}) collective-permute-start(f32[2,64,128]{2,1,0:T(8,128)S(1)} %constant_dynamic-slice_fusion), channel_id=1, source_target_pairs={{0,4},{4,0},{1,5},{5,1},{2,6},{6,2},{3,7},{7,3},{8,12},{12,8},{9,1... | collective-permute-start | bytes 196616 | tf_op jit(solution)/shard_map/ppermute | solution.py:427
  222.2 8.4 %collective-permute-start.19 = (bf16[144,768]{1,0:T(8,128)(2,1)S(1)}, bf16[144,768]{1,0:T(8,128)(2,1)S(1)}, u32[]{:S(2)}, u32[]{:S(2)}) collective-permute-start(bf16[144,768]{1,0:T(8,128)(2,1)S(1)} %get-tuple-element.53.rest_0_), channel_id=1, source_target_pairs={{0,8},{8,0},{16,24},{24,16},{1,9},{9,1},{17,25},{25,17},{2,10},{10... | collective-permute-start | bytes 663560 | tf_op jit(solution)/shard_map/ppermute | solution.py:308
  222.8 14.6 %collective-permute-start.20 = (bf16[144,768]{1,0:T(8,128)(2,1)S(1)}, bf16[144,768]{1,0:T(8,128)(2,1)S(1)}, u32[]{:S(2)}, u32[]{:S(2)}) collective-permute-start(bf16[144,768]{1,0:T(8,128)(2,1)S(1)} %get-tuple-element.53.rest_0_), channel_id=1, source_target_pairs={{0,16},{8,24},{16,0},{24,8},{1,17},{9,25},{17,1},{25,9},{2,18},{10... | collective-permute-start | bytes 663560 | tf_op jit(solution)/shard_map/ppermute | solution.py:308
  224.0 14.6 %collective-permute-start.21 = (bf16[144,768]{1,0:T(8,128)(2,1)S(1)}, bf16[144,768]{1,0:T(8,128)(2,1)S(1)}, u32[]{:S(2)}, u32[]{:S(2)}) collective-permute-start(bf16[144,768]{1,0:T(8,128)(2,1)S(1)} %get-tuple-element.53.rest_0_), channel_id=1, source_target_pairs={{0,24},{8,16},{16,8},{24,0},{1,25},{9,17},{17,9},{25,1},{2,26},{10... | collective-permute-start | bytes 663560 | tf_op jit(solution)/shard_map/ppermute | solution.py:308
  225.8 16.4 %collective-permute-start.11 = (bf16[144,256]{1,0:T(8,128)(2,1)S(1)}, bf16[144,256]{1,0:T(8,128)(2,1)S(1)}, u32[]{:S(2)}, u32[]{:S(2)}) collective-permute-start(bf16[144,256]{1,0:T(8,128)(2,1)S(1)} %get-tuple-element.44.rest_0_), channel_id=1, source_target_pairs={{0,16},{8,24},{16,0},{24,8},{1,17},{9,25},{17,1},{25,9},{2,18},{10... | collective-permute-start | bytes 221192 | tf_op jit(solution)/shard_map/ppermute | solution.py:308
  226.3 16.0 %collective-permute-start.12 = (bf16[144,256]{1,0:T(8,128)(2,1)S(1)}, bf16[144,256]{1,0:T(8,128)(2,1)S(1)}, u32[]{:S(2)}, u32[]{:S(2)}) collective-permute-start(bf16[144,256]{1,0:T(8,128)(2,1)S(1)} %get-tuple-element.44.rest_0_), channel_id=1, source_target_pairs={{0,24},{8,16},{16,8},{24,0},{1,25},{9,17},{17,9},{25,1},{2,26},{10... | collective-permute-start | bytes 221192 | tf_op jit(solution)/shard_map/ppermute | solution.py:308
  230.6 13.4 %collective-permute-start.26 = (f32[2,64,128]{2,1,0:T(8,128)S(1)}, f32[2,64,128]{2,1,0:T(8,128)S(1)}, u32[]{:S(2)}, u32[]{:S(2)}) collective-permute-start(f32[2,64,128]{2,1,0:T(8,128)S(1)} %add_subtract_fusion), channel_id=1, source_target_pairs={{0,8},{8,0},{16,24},{24,16},{1,9},{9,1},{17,25},{25,17},{2,10},{10... | collective-permute-start | bytes 196616 | tf_op jit(solution)/shard_map/ppermute | solution.py:308
  237.4 6.6 %collective-permute-start.27 = (f32[2,64,128]{2,1,0:T(8,128)S(1)}, f32[2,64,128]{2,1,0:T(8,128)S(1)}, u32[]{:S(2)}, u32[]{:S(2)}) collective-permute-start(f32[2,64,128]{2,1,0:T(8,128)S(1)} %add_subtract_fusion), channel_id=1, source_target_pairs={{0,16},{8,24},{16,0},{24,8},{1,17},{9,25},{17,1},{25,9},{2,18},{10... | collective-permute-start | bytes 196616 | tf_op jit(solution)/shard_map/ppermute | solution.py:308
  238.7 5.4 %collective-permute-start.28 = (f32[2,64,128]{2,1,0:T(8,128)S(1)}, f32[2,64,128]{2,1,0:T(8,128)S(1)}, u32[]{:S(2)}, u32[]{:S(2)}) collective-permute-start(f32[2,64,128]{2,1,0:T(8,128)S(1)} %add_subtract_fusion), channel_id=1, source_target_pairs={{0,24},{8,16},{16,8},{24,0},{1,25},{9,17},{17,9},{25,1},{2,26},{10... | collective-permute-start | bytes 196616 | tf_op jit(solution)/shard_map/ppermute | solution.py:308
  (14 other events, 17.2 us)

commit v4 on v3

--- a/solution.py
+++ b/solution.py
@@ -160,6 +160,10 @@
     )(scalars, own, *received)
 
 
+def far(x):
+    return pltpu.with_memory_space_constraint(x, pltpu.HBM)
+
+
 def gathered(u_refs, all_ref, owner_ref, at):
     for k, ref in enumerate(u_refs):
         all_ref[owner_ref[at + k]] = ref[...]
@@ -186,7 +190,7 @@
         shared_ref[n] += dot_nt(hi[rows], u[n]) + dot_nt(lo[rows], u[n])
 
 
-def col_call(tile, nodes, scalars, at, own, received, u, first):
+def col_call(tile, nodes, scalars, at, own, received, u, first, last):
     part, width = own.shape
     block = lambda rows: pl.BlockSpec((rows, tile), lambda j, w: (0, j))
     some = u[0].shape[1]
@@ -205,7 +209,7 @@
         out_shape=[shared, jax.ShapeDtypeStruct((part + PAD, width), BF16)],
         compiler_params=pltpu.CompilerParams(vmem_limit_bytes=16 << 20),
         name="col_sum",
-    )(scalars, own, *u, *received)
+    )(scalars, own, *(far(x) for x in u), *(received if last else [far(x) for x in received]))
 
 
 def place_body(n_in, at, at_ref, *rest):
@@ -408,7 +412,8 @@
             for k, x in enumerate(parts):
                 received.append(send(x, "col", k + 1, n_col))
             projected, payload = col_call(
-                tile, nodes, scalars, owners, own, received, upper, rows + firsts[g]
+                tile, nodes, scalars, owners, own, received, upper, rows + firsts[g],
+                g == len(widths) - 1,
             )
             shared.append(projected)
             payloads = [payload]

time: 245 us -> 237 us (0.967)
  local copies, waits for them, and re-layouts: 11.8 us -> 2.9 us
    unnamed x34 -> x14, local copies, waits for them, and re-layouts: 9.67 us -> 0.74 us
  transfers between devices with their start and end apart: 29 -> 29, of which waited for: 9 -> 11; matrix products, arithmetic and copies ran while one was open for 3% -> 3% of each run, Pallas kernels for 40% -> 42%
where the time goes in v4:
time: 237 us
  Pallas kernels  98.2 us (41%)
  waiting for transfers between devices  91.2 us (38%)
  starting transfers between devices  35.8 us (15%)
  other arithmetic  6.9 us (3%)
  local copies, waits for them, and re-layouts  2.9 us (1%)
    pallas_call x4, Pallas kernels, main_call(): pl.pallas_call(functools.partial(main_body, outs, steps, halves, nodes),...  76.9 us
    ppermute x3, waiting for transfers between devices, per_device(): upper.append(lax.ppermute(upper[-1], 'col', ring))  57.4 us
    ppermute x24, waiting for transfers between devices, send(): return lax.ppermute(x, axis, [(i, peer(i, k, n)) for i in range(n)])  33.8 us
    ppermute x24, starting transfers between devices, send(): return lax.ppermute(x, axis, [(i, peer(i, k, n)) for i in range(n)])  32.6 us
    pallas_call x1, Pallas kernels, project_call(): pl.pallas_call(functools.partial(project_body, halves, nodes, per_col, n_...  6.52 us
    pallas_call x2, Pallas kernels, pole_call(): pl.pallas_call(functools.partial(pole_body, nodes, per_col, len(received)...  5.85 us
    pallas_call x2, Pallas kernels, col_call(): pl.pallas_call(functools.partial(col_body, nodes, len(u), at), grid_spec=...  5.74 us
  transfers between devices with their start and end apart: 29, of which 11 were waited for; matrix products, arithmetic and copies ran while one was open for 3% of the time, Pallas kernels for 42%

profile of v4, /device:TPU:0, one launch (start us, length us, event | category | flops | bytes accessed | tf_op | source)
XLA Modules:
  0.0 236.7 jit_solution(8542526062704341977)
XLA Ops:
  0.6 1.8 slice_bitcast_fusion
  2.6 3.1 %collective-permute-start.4 = (bf16[2,64,5120]{2,1,0:T(8,128)(2,1)S(1)}, bf16[2,64,5120]{2,1,0:T(8,128)(2,1)S(1)}, u32[]{:S(2)}, u32[]{:S(2)}) collective-permute-start(bf16[2,64,5120]{2,1,0:T(8,128)(2,1)S(1)} %pad_maximum_fusion.1.rest_0_), channel_id=1, source_target_pairs={{0,1},{1,2},{2,3},{3,0},{4,5},{5,6},{6,7},{7,4},{8,9},{9,10},{10,1... | collective-permute-start | bytes 3932168 | tf_op jit(solution)/shard_map/ppermute | solution.py:389
  5.7 30.8 %collective-permute-done.4.rest_1_ = bf16[2,64,5120]{2,1,0:T(8,128)(2,1)S(1)} collective-permute-done((bf16[2,64,5120]{2,1,0:T(8,128)(2,1)S(1)}, bf16[2,64,5120]{2,1,0:T(8,128)(2,1)S(1)}, u32[]{:S(2)}, u32[]{:S(2)}) %collective-permute-start.4) | collective-permute-done | bytes 1310752 | tf_op jit(solution)/shard_map/ppermute | solution.py:389
  39.1 2.6 %pad_maximum_fusion = bf16[2,2,2,128,2048]{4,3,2,1,0:T(8,128)(2,1)S(1)} fusion(bf16[1,2,2,128,2048]{4,3,2,1,0:T(8,128)(2,1)} %bitcast.41, bf16[1,2,2,128,2048]{4,3,2,1,0:T(8,128)(2,1)} %bitcast.40), kind=kLoop, calls=%fused_computation | loop fusion | flops 2097152 | bytes 8388608 | tf_op jit(solution)/shard_map/stack | solution.py:341
  41.7 26.6 %collective-permute-done.5.rest_2_ = bf16[2,64,5120]{2,1,0:T(8,128)(2,1)} collective-permute-done((bf16[2,64,5120]{2,1,0:T(8,128)(2,1)S(1)}, bf16[2,64,5120]{2,1,0:T(8,128)(2,1)}, u32[]{:S(2)}, u32[]{:S(2)}) %collective-permute-start.5) | collective-permute-done | bytes 1310752 | tf_op jit(solution)/shard_map/ppermute | solution.py:389
  68.3 2.0 bitcast_convert_fusion.rest_1_
  70.3 27.5 %products.4 = (f32[512,4096]{1,0:T(8,128)S(1)}, bf16[528,768]{1,0:T(8,128)(2,1)S(1)}, bf16[528,768]{1,0:T(8,128)(2,1)S(1)}) custom-call(s32[36]{0:T(128)S(1)} %stack.156.base_ref.where_ref.owner_ref.at_ref, f32[5]{0:T(128)S(1)} %pad_maximum_fusion.2.w_ref, bf16[2,2,4096,2048]{3,2,1,0:T(8,128)(2,1)} %g_ref.7, bf16[1024,2048]{1,0:T(8,128)(2,1)S(1)} %bitcast.65, ...), custom_call_target="tpu_custom_call" | custom-call | tf_op jit(solution)/shard_map/products/pallas_call | solution.py:116
  97.9 27.6 %products.5 = (f32[512,4096]{1,0:T(8,128)S(1)}, bf16[528,768]{1,0:T(8,128)(2,1)S(1)}, f32[512,768]{1,0:T(8,128)S(1)}) custom-call(s32[36]{0:T(128)S(1)} %stack.156.base_ref.where_ref.owner_ref.at_ref, f32[5]{0:T(128)S(1)} %pad_maximum_fusion.2.w_ref, bf16[2,2,4096,2048]{3,2,1,0:T(8,128)(2,1)} %g_ref.7, ...), custom_call_target="tpu_custom_call", output_to_operand_aliasing={{0}: (5, {})} | custom-call | tf_op jit(solution)/shard_map/products/pallas_call | solution.py:116
  126.8 1.5 collective-permute-start.14
  129.0 15.2 %products.6 = (f32[512,4096]{1,0:T(8,128)S(1)}, bf16[528,256]{1,0:T(8,128)(2,1)S(1)}, bf16[528,256]{1,0:T(8,128)(2,1)S(1)}, bf16[528,256]{1,0:T(8,128)(2,1)S(1)}) custom-call(s32[36]{0:T(128)S(1)} %stack.156.base_ref.where_ref.owner_ref.at_ref, f32[5]{0:T(128)S(1)} %pad_maximum_fusion.2.w_ref, ...), custom_call_target="tpu_custom_call", output_to_operand_aliasing={{0}: (5, {})} | custom-call | tf_op jit(solution)/shard_map/products/pallas_call | solution.py:116
  147.8 14.2 %collective-permute-done.14.rest_1_ = bf16[528,768]{1,0:T(8,128)(2,1)S(1)} collective-permute-done((bf16[528,768]{1,0:T(8,128)(2,1)S(1)}, bf16[528,768]{1,0:T(8,128)(2,1)S(1)}, u32[]{:S(2)}, u32[]{:S(2)}) %collective-permute-start.14) | collective-permute-done | bytes 811040 | tf_op jit(solution)/shard_map/ppermute | solution.py:312
  162.0 1.6 collective-permute-start.3
  164.6 4.4 %pole_sum.3 = (f32[128,768]{1,0:T(8,128)S(1)}, bf16[144,768]{1,0:T(8,128)(2,1)S(1)}, bf16[144,768]{1,0:T(8,128)(2,1)}, bf16[144,768]{1,0:T(8,128)(2,1)}) custom-call(s32[36]{0:T(128)S(1)} %stack.156.base_ref.where_ref.owner_ref.at_ref, f32[512,768]{1,0:T(8,128)S(1)} %get-tuple-element.45.own_ref, bf16[528,768]{1,0:T(8,128)(2,1)S(1)} %collective-permute-done.13.rest_0_, ...), custom_call_target="tpu_custom_call" | custom-call | tf_op jit(solution)/shard_map/pole_sum/pallas_call | solution.py:147
  169.0 6.6 %products.7 = (f32[512,4096]{1,0:T(8,128)S(1)}, f32[512,256]{1,0:T(8,128)S(1)}) custom-call(s32[36]{0:T(128)S(1)} %stack.156.base_ref.where_ref.owner_ref.at_ref, f32[5]{0:T(128)S(1)} %pad_maximum_fusion.2.w_ref, bf16[2,2,4096,2048]{3,2,1,0:T(8,128)(2,1)} %g_ref.7, bf16[1024,2048]{1,0:T(8,128)(2,1)S(1)} %bitcast.68, ...), custom_call_target="tpu_custom_call", output_to_operand_aliasing={{0}: (5, {})} | custom-call | tf_op jit(solution)/shard_map/products/pallas_call | solution.py:116
  175.6 1.5 pole_sum.2
  177.1 2.1 collective-permute-start.7
  179.2 2.4 %collective-permute-start.17 = (bf16[144,768]{1,0:T(8,128)(2,1)}, bf16[144,768]{1,0:T(8,128)(2,1)}, u32[]{:S(2)}, u32[]{:S(2)}) collective-permute-start(bf16[144,768]{1,0:T(8,128)(2,1)} %get-tuple-element.51), channel_id=1, source_target_pairs={{0,2},{1,3},{2,0},{3,1},{4,6},{5,7},{6,4},{7,5},{8,10},{9,11},{10,... | collective-permute-start | bytes 663560 | tf_op jit(solution)/shard_map/ppermute | solution.py:312
  183.7 2.2 collective-permute-start.8
  186.7 6.5 %project.1 = (f32[2,64,256]{2,1,0:T(8,128)S(1)}, f32[2,64,256]{2,1,0:T(8,128)}, f32[2,64,256]{2,1,0:T(8,128)}, f32[2,64,256]{2,1,0:T(8,128)}) custom-call(s32[36]{0:T(128)S(1)} %stack.156.base_ref.where_ref.owner_ref.at_ref, f32[512,4096]{1,0:T(8,128)S(1)} %get-tuple-element.57.z_ref, bf16[2,64,5120]{2,1,0:T(8,128)(2,1)S(1)} %pad_maximum_fusion.1.rest_0_, ...), custom_call_target="tpu_custom_call" | custom-call | tf_op jit(solution)/shard_map/project/pallas_call | solution.py:282
  193.3 8.2 %collective-permute-done.8.rest_5_ = bf16[144,256]{1,0:T(8,128)(2,1)S(1)} collective-permute-done((bf16[144,256]{1,0:T(8,128)(2,1)S(1)}, bf16[144,256]{1,0:T(8,128)(2,1)S(1)}, u32[]{:S(2)}, u32[]{:S(2)}) %collective-permute-start.8) | collective-permute-done | bytes 73760 | tf_op jit(solution)/shard_map/ppermute | solution.py:312
  201.9 3.3 %collective-permute-start.23 = (f32[2,64,256]{2,1,0:T(8,128)}, f32[2,64,256]{2,1,0:T(8,128)S(1)}, u32[]{:S(2)}, u32[]{:S(2)}) collective-permute-start(f32[2,64,256]{2,1,0:T(8,128)} %get-tuple-element.60), channel_id=1, source_target_pairs={{0,2},{1,3},{2,0},{3,1},{4,6},{5,7},{6,4},{7,5},{8,10},{9,11},{10,... | collective-permute-start | bytes 393224 | tf_op jit(solution)/shard_map/ppermute | solution.py:312
  206.5 1.8 col_sum.2
  208.4 1.6 collective-permute-start.10
  209.9 3.9 %col_sum.3 = (f32[2,64,256]{2,1,0:T(8,128)S(1)}, bf16[144,768]{1,0:T(8,128)(2,1)S(1)}) custom-call(s32[36]{0:T(128)S(1)} %stack.156.base_ref.where_ref.owner_ref.at_ref, f32[128,768]{1,0:T(8,128)S(1)} %get-tuple-element.49.own_ref, bf16[2,64,5120]{2,1,0:T(8,128)(2,1)} %copy-done, bf16[2,64,5120]{2,1,0:T(8,128)(2,1)} %copy-done.1, ...), custom_call_target="tpu_custom_call" | custom-call | tf_op jit(solution)/shard_map/col_sum/pallas_call | solution.py:198
  214.2 1.6 collective-permute-start.19
  216.3 1.5 collective-permute-start.21
  218.9 1.8 collective-permute-start.12
  220.8 1.8 collective-permute-done.19.rest_1_
  222.6 1.5 collective-permute-start.26
  224.1 6.3 %collective-permute-done.20.rest_2_ = bf16[144,768]{1,0:T(8,128)(2,1)S(1)} collective-permute-done((bf16[144,768]{1,0:T(8,128)(2,1)S(1)}, bf16[144,768]{1,0:T(8,128)(2,1)S(1)}, u32[]{:S(2)}, u32[]{:S(2)}) %collective-permute-start.20) | collective-permute-done | bytes 221216 | tf_op jit(solution)/shard_map/ppermute | solution.py:312
  230.9 1.5 collective-permute-start.28
  232.4 1.8 place.2.rest_4_
  (67 shorter events, 18.2 us)
Async XLA Ops:
  2.4 35.9 %copy-start.3 = (f32[2,2,2,128,64]{3,4,2,1,0:T(8,128)S(1)}, f32[2,2,2,128,64]{3,4,2,1,0:T(8,128)}, u32[]{:S(2)}) copy-start(f32[2,2,2,128,64]{3,4,2,1,0:T(8,128)} %param.8) | copy-start | bytes 786436
  2.6 184.2 %copy-start = (bf16[2,64,5120]{2,1,0:T(8,128)(2,1)}, bf16[2,64,5120]{2,1,0:T(8,128)(2,1)S(1)}, u32[]{:S(2)}) copy-start(bf16[2,64,5120]{2,1,0:T(8,128)(2,1)S(1)} %pad_maximum_fusion.1.rest_0_) | copy-start | bytes 3932164
  2.6 33.9 %collective-permute-start.4 = (bf16[2,64,5120]{2,1,0:T(8,128)(2,1)S(1)}, bf16[2,64,5120]{2,1,0:T(8,128)(2,1)S(1)}, u32[]{:S(2)}, u32[]{:S(2)}) collective-permute-start(bf16[2,64,5120]{2,1,0:T(8,128)(2,1)S(1)} %pad_maximum_fusion.1.rest_0_), channel_id=1, source_target_pairs={{0,1},{1,2},{2,3},{3,0},{4,5},{5,6},{6,7},{7,4},{8,9},{9,10},{10,1... | collective-permute-start | bytes 3932168 | tf_op jit(solution)/shard_map/ppermute | solution.py:389
  5.7 33.4 %collective-permute-start = (bf16[2,2,128,2048]{3,2,1,0:T(8,128)(2,1)}, bf16[2,2,128,2048]{3,2,1,0:T(8,128)(2,1)}, u32[]{:S(2)}, u32[]{:S(2)}) collective-permute-start(bf16[2,2,128,2048]{3,2,1,0:T(8,128)(2,1)} %param.6), channel_id=1, source_target_pairs={{0,4},{4,0},{1,5},{5,1},{2,6},{6,2},{3,7},{7,3},{8,12},{12,8},{9,1... | collective-permute-start | bytes 6291464 | tf_op jit(solution)/shard_map/ppermute | solution.py:340
  36.5 150.3 %copy-start.1 = (bf16[2,64,5120]{2,1,0:T(8,128)(2,1)}, bf16[2,64,5120]{2,1,0:T(8,128)(2,1)S(1)}, u32[]{:S(2)}) copy-start(bf16[2,64,5120]{2,1,0:T(8,128)(2,1)S(1)} %collective-permute-done.4.rest_1_) | copy-start | bytes 3932164
  36.5 31.8 %collective-permute-start.5 = (bf16[2,64,5120]{2,1,0:T(8,128)(2,1)S(1)}, bf16[2,64,5120]{2,1,0:T(8,128)(2,1)}, u32[]{:S(2)}, u32[]{:S(2)}) collective-permute-start(bf16[2,64,5120]{2,1,0:T(8,128)(2,1)S(1)} %collective-permute-done.4.rest_1_), channel_id=1, source_target_pairs={{0,1},{1,2},{2,3},{3,0},{4,5},{5,6},{6,7},{7,4},{8,9},{9,10},{10,1... | collective-permute-start | bytes 3932168 | tf_op jit(solution)/shard_map/ppermute | solution.py:389
  68.3 117.6 %collective-permute-start.6 = (bf16[2,64,5120]{2,1,0:T(8,128)(2,1)}, bf16[2,64,5120]{2,1,0:T(8,128)(2,1)S(1)}, u32[]{:S(2)}, u32[]{:S(2)}) collective-permute-start(bf16[2,64,5120]{2,1,0:T(8,128)(2,1)} %collective-permute-done.5.rest_2_), channel_id=1, source_target_pairs={{0,1},{1,2},{2,3},{3,0},{4,5},{5,6},{6,7},{7,4},{8,9},{9,10},{10,1... | collective-permute-start | bytes 3932168 | tf_op jit(solution)/shard_map/ppermute | solution.py:389
  125.5 21.0 %collective-permute-start.13 = (bf16[528,768]{1,0:T(8,128)(2,1)S(1)}, bf16[528,768]{1,0:T(8,128)(2,1)S(1)}, u32[]{:S(2)}, u32[]{:S(2)}) collective-permute-start(bf16[528,768]{1,0:T(8,128)(2,1)S(1)} %get-tuple-element.46), channel_id=1, source_target_pairs={{0,8},{8,0},{16,24},{24,16},{1,9},{9,1},{17,25},{25,17},{2,10},{10... | collective-permute-start | bytes 2433032 | tf_op jit(solution)/shard_map/ppermute | solution.py:312
  126.8 35.2 %collective-permute-start.14 = (bf16[528,768]{1,0:T(8,128)(2,1)S(1)}, bf16[528,768]{1,0:T(8,128)(2,1)S(1)}, u32[]{:S(2)}, u32[]{:S(2)}) collective-permute-start(bf16[528,768]{1,0:T(8,128)(2,1)S(1)} %get-tuple-element.47), channel_id=1, source_target_pairs={{0,16},{8,24},{16,0},{24,8},{1,17},{9,25},{17,1},{25,9},{2,18},{10... | collective-permute-start | bytes 2433032 | tf_op jit(solution)/shard_map/ppermute | solution.py:312
  128.3 36.3 %collective-permute-start.15 = (bf16[528,768]{1,0:T(8,128)(2,1)S(1)}, bf16[528,768]{1,0:T(8,128)(2,1)S(1)}, u32[]{:S(2)}, u32[]{:S(2)}) collective-permute-start(bf16[528,768]{1,0:T(8,128)(2,1)S(1)} %get-tuple-element.48), channel_id=1, source_target_pairs={{0,24},{8,16},{16,8},{24,0},{1,25},{9,17},{17,9},{25,1},{2,26},{10... | collective-permute-start | bytes 2433032 | tf_op jit(solution)/shard_map/ppermute | solution.py:312
  144.2 31.4 %collective-permute-start.1 = (bf16[528,256]{1,0:T(8,128)(2,1)S(1)}, bf16[528,256]{1,0:T(8,128)(2,1)S(1)}, u32[]{:S(2)}, u32[]{:S(2)}) collective-permute-start(bf16[528,256]{1,0:T(8,128)(2,1)S(1)} %get-tuple-element.37), channel_id=1, source_target_pairs={{0,8},{8,0},{16,24},{24,16},{1,9},{9,1},{17,25},{25,17},{2,10},{10... | collective-permute-start | bytes 811016 | tf_op jit(solution)/shard_map/ppermute | solution.py:312
  146.5 29.1 %collective-permute-start.2 = (bf16[528,256]{1,0:T(8,128)(2,1)S(1)}, bf16[528,256]{1,0:T(8,128)(2,1)S(1)}, u32[]{:S(2)}, u32[]{:S(2)}) collective-permute-start(bf16[528,256]{1,0:T(8,128)(2,1)S(1)} %get-tuple-element.38), channel_id=1, source_target_pairs={{0,16},{8,24},{16,0},{24,8},{1,17},{9,25},{17,1},{25,9},{2,18},{10... | collective-permute-start | bytes 811016 | tf_op jit(solution)/shard_map/ppermute | solution.py:312
  162.0 13.6 %collective-permute-start.3 = (bf16[528,256]{1,0:T(8,128)(2,1)S(1)}, bf16[528,256]{1,0:T(8,128)(2,1)S(1)}, u32[]{:S(2)}, u32[]{:S(2)}) collective-permute-start(bf16[528,256]{1,0:T(8,128)(2,1)S(1)} %get-tuple-element.39), channel_id=1, source_target_pairs={{0,24},{8,16},{16,8},{24,0},{1,25},{9,17},{17,9},{25,1},{2,26},{10... | collective-permute-start | bytes 811016 | tf_op jit(solution)/shard_map/ppermute | solution.py:312
  169.0 36.2 %collective-permute-start.16 = (bf16[144,768]{1,0:T(8,128)(2,1)S(1)}, bf16[144,768]{1,0:T(8,128)(2,1)S(1)}, u32[]{:S(2)}, u32[]{:S(2)}) collective-permute-start(bf16[144,768]{1,0:T(8,128)(2,1)S(1)} %get-tuple-element.50), channel_id=1, source_target_pairs={{0,1},{1,0},{2,3},{3,2},{4,5},{5,4},{6,7},{7,6},{8,9},{9,8},{10,11... | collective-permute-start | bytes 663560 | tf_op jit(solution)/shard_map/ppermute | solution.py:312
  177.1 6.6 %collective-permute-start.7 = (bf16[144,256]{1,0:T(8,128)(2,1)S(1)}, bf16[144,256]{1,0:T(8,128)(2,1)S(1)}, u32[]{:S(2)}, u32[]{:S(2)}) collective-permute-start(bf16[144,256]{1,0:T(8,128)(2,1)S(1)} %get-tuple-element.41), channel_id=1, source_target_pairs={{0,1},{1,0},{2,3},{3,2},{4,5},{5,4},{6,7},{7,6},{8,9},{9,8},{10,11... | collective-permute-start | bytes 221192 | tf_op jit(solution)/shard_map/ppermute | solution.py:312
  179.2 29.1 %collective-permute-start.17 = (bf16[144,768]{1,0:T(8,128)(2,1)}, bf16[144,768]{1,0:T(8,128)(2,1)}, u32[]{:S(2)}, u32[]{:S(2)}) collective-permute-start(bf16[144,768]{1,0:T(8,128)(2,1)} %get-tuple-element.51), channel_id=1, source_target_pairs={{0,2},{1,3},{2,0},{3,1},{4,6},{5,7},{6,4},{7,5},{8,10},{9,11},{10,... | collective-permute-start | bytes 663560 | tf_op jit(solution)/shard_map/ppermute | solution.py:312
  181.7 28.3 %collective-permute-start.18 = (bf16[144,768]{1,0:T(8,128)(2,1)}, bf16[144,768]{1,0:T(8,128)(2,1)}, u32[]{:S(2)}, u32[]{:S(2)}) collective-permute-start(bf16[144,768]{1,0:T(8,128)(2,1)} %get-tuple-element.52), channel_id=1, source_target_pairs={{0,3},{1,2},{2,1},{3,0},{4,7},{5,6},{6,5},{7,4},{8,11},{9,10},{10,... | collective-permute-start | bytes 663560 | tf_op jit(solution)/shard_map/ppermute | solution.py:312
  183.7 17.7 %collective-permute-start.8 = (bf16[144,256]{1,0:T(8,128)(2,1)S(1)}, bf16[144,256]{1,0:T(8,128)(2,1)S(1)}, u32[]{:S(2)}, u32[]{:S(2)}) collective-permute-start(bf16[144,256]{1,0:T(8,128)(2,1)S(1)} %get-tuple-element.42), channel_id=1, source_target_pairs={{0,2},{1,3},{2,0},{3,1},{4,6},{5,7},{6,4},{7,5},{8,10},{9,11},{10,... | collective-permute-start | bytes 221192 | tf_op jit(solution)/shard_map/ppermute | solution.py:312
  185.9 15.9 %collective-permute-start.9 = (bf16[144,256]{1,0:T(8,128)(2,1)S(1)}, bf16[144,256]{1,0:T(8,128)(2,1)S(1)}, u32[]{:S(2)}, u32[]{:S(2)}) collective-permute-start(bf16[144,256]{1,0:T(8,128)(2,1)S(1)} %get-tuple-element.43), channel_id=1, source_target_pairs={{0,3},{1,2},{2,1},{3,0},{4,7},{5,6},{6,5},{7,4},{8,11},{9,10},{10,... | collective-permute-start | bytes 221192 | tf_op jit(solution)/shard_map/ppermute | solution.py:312
  201.4 12.4 %collective-permute-start.22 = (f32[2,64,256]{2,1,0:T(8,128)}, f32[2,64,256]{2,1,0:T(8,128)S(1)}, u32[]{:S(2)}, u32[]{:S(2)}) collective-permute-start(f32[2,64,256]{2,1,0:T(8,128)} %get-tuple-element.59), channel_id=1, source_target_pairs={{0,1},{1,0},{2,3},{3,2},{4,5},{5,4},{6,7},{7,6},{8,9},{9,8},{10,11... | collective-permute-start | bytes 393224 | tf_op jit(solution)/shard_map/ppermute | solution.py:312
  201.9 12.2 %collective-permute-start.23 = (f32[2,64,256]{2,1,0:T(8,128)}, f32[2,64,256]{2,1,0:T(8,128)S(1)}, u32[]{:S(2)}, u32[]{:S(2)}) collective-permute-start(f32[2,64,256]{2,1,0:T(8,128)} %get-tuple-element.60), channel_id=1, source_target_pairs={{0,2},{1,3},{2,0},{3,1},{4,6},{5,7},{6,4},{7,5},{8,10},{9,11},{10,... | collective-permute-start | bytes 393224 | tf_op jit(solution)/shard_map/ppermute | solution.py:312
  205.9 8.1 %collective-permute-start.24 = (f32[2,64,256]{2,1,0:T(8,128)}, f32[2,64,256]{2,1,0:T(8,128)S(1)}, u32[]{:S(2)}, u32[]{:S(2)}) collective-permute-start(f32[2,64,256]{2,1,0:T(8,128)} %get-tuple-element.61), channel_id=1, source_target_pairs={{0,3},{1,2},{2,1},{3,0},{4,7},{5,6},{6,5},{7,4},{8,11},{9,10},{10,... | collective-permute-start | bytes 393224 | tf_op jit(solution)/shard_map/ppermute | solution.py:312
  208.4 9.4 %collective-permute-start.10 = (bf16[144,256]{1,0:T(8,128)(2,1)S(1)}, bf16[144,256]{1,0:T(8,128)(2,1)S(1)}, u32[]{:S(2)}, u32[]{:S(2)}) collective-permute-start(bf16[144,256]{1,0:T(8,128)(2,1)S(1)} %get-tuple-element.44.rest_0_), channel_id=1, source_target_pairs={{0,8},{8,0},{16,24},{24,16},{1,9},{9,1},{17,25},{25,17},{2,10},{10... | collective-permute-start | bytes 221192 | tf_op jit(solution)/shard_map/ppermute | solution.py:312
  214.1 4.8 %collective-permute-start.25 = (f32[2,64,128]{2,1,0:T(8,128)S(1)}, f32[2,64,128]{2,1,0:T(8,128)S(1)}, u32[]{:S(2)}, u32[]{:S(2)}) collective-permute-start(f32[2,64,128]{2,1,0:T(8,128)S(1)} %constant_dynamic-slice_fusion), channel_id=1, source_target_pairs={{0,4},{4,0},{1,5},{5,1},{2,6},{6,2},{3,7},{7,3},{8,12},{12,8},{9,1... | collective-permute-start | bytes 196616 | tf_op jit(solution)/shard_map/ppermute | solution.py:432
  214.2 8.4 %collective-permute-start.19 = (bf16[144,768]{1,0:T(8,128)(2,1)S(1)}, bf16[144,768]{1,0:T(8,128)(2,1)S(1)}, u32[]{:S(2)}, u32[]{:S(2)}) collective-permute-start(bf16[144,768]{1,0:T(8,128)(2,1)S(1)} %get-tuple-element.53.rest_0_), channel_id=1, source_target_pairs={{0,8},{8,0},{16,24},{24,16},{1,9},{9,1},{17,25},{25,17},{2,10},{10... | collective-permute-start | bytes 663560 | tf_op jit(solution)/shard_map/ppermute | solution.py:312
  215.8 14.6 %collective-permute-start.20 = (bf16[144,768]{1,0:T(8,128)(2,1)S(1)}, bf16[144,768]{1,0:T(8,128)(2,1)S(1)}, u32[]{:S(2)}, u32[]{:S(2)}) collective-permute-start(bf16[144,768]{1,0:T(8,128)(2,1)S(1)} %get-tuple-element.53.rest_0_), channel_id=1, source_target_pairs={{0,16},{8,24},{16,0},{24,8},{1,17},{9,25},{17,1},{25,9},{2,18},{10... | collective-permute-start | bytes 663560 | tf_op jit(solution)/shard_map/ppermute | solution.py:312
  216.3 14.6 %collective-permute-start.21 = (bf16[144,768]{1,0:T(8,128)(2,1)S(1)}, bf16[144,768]{1,0:T(8,128)(2,1)S(1)}, u32[]{:S(2)}, u32[]{:S(2)}) collective-permute-start(bf16[144,768]{1,0:T(8,128)(2,1)S(1)} %get-tuple-element.53.rest_0_), channel_id=1, source_target_pairs={{0,24},{8,16},{16,8},{24,0},{1,25},{9,17},{17,9},{25,1},{2,26},{10... | collective-permute-start | bytes 663560 | tf_op jit(solution)/shard_map/ppermute | solution.py:312
  217.8 16.4 %collective-permute-start.11 = (bf16[144,256]{1,0:T(8,128)(2,1)S(1)}, bf16[144,256]{1,0:T(8,128)(2,1)S(1)}, u32[]{:S(2)}, u32[]{:S(2)}) collective-permute-start(bf16[144,256]{1,0:T(8,128)(2,1)S(1)} %get-tuple-element.44.rest_0_), channel_id=1, source_target_pairs={{0,16},{8,24},{16,0},{24,8},{1,17},{9,25},{17,1},{25,9},{2,18},{10... | collective-permute-start | bytes 221192 | tf_op jit(solution)/shard_map/ppermute | solution.py:312
  218.9 15.3 %collective-permute-start.12 = (bf16[144,256]{1,0:T(8,128)(2,1)S(1)}, bf16[144,256]{1,0:T(8,128)(2,1)S(1)}, u32[]{:S(2)}, u32[]{:S(2)}) collective-permute-start(bf16[144,256]{1,0:T(8,128)(2,1)S(1)} %get-tuple-element.44.rest_0_), channel_id=1, source_target_pairs={{0,24},{8,16},{16,8},{24,0},{1,25},{9,17},{17,9},{25,1},{2,26},{10... | collective-permute-start | bytes 221192 | tf_op jit(solution)/shard_map/ppermute | solution.py:312
  222.6 13.1 %collective-permute-start.26 = (f32[2,64,128]{2,1,0:T(8,128)S(1)}, f32[2,64,128]{2,1,0:T(8,128)S(1)}, u32[]{:S(2)}, u32[]{:S(2)}) collective-permute-start(f32[2,64,128]{2,1,0:T(8,128)S(1)} %add_subtract_fusion), channel_id=1, source_target_pairs={{0,8},{8,0},{16,24},{24,16},{1,9},{9,1},{17,25},{25,17},{2,10},{10... | collective-permute-start | bytes 196616 | tf_op jit(solution)/shard_map/ppermute | solution.py:312
  230.4 5.3 %collective-permute-start.27 = (f32[2,64,128]{2,1,0:T(8,128)S(1)}, f32[2,64,128]{2,1,0:T(8,128)S(1)}, u32[]{:S(2)}, u32[]{:S(2)}) collective-permute-start(f32[2,64,128]{2,1,0:T(8,128)S(1)} %add_subtract_fusion), channel_id=1, source_target_pairs={{0,16},{8,24},{16,0},{24,8},{1,17},{9,25},{17,1},{25,9},{2,18},{10... | collective-permute-start | bytes 196616 | tf_op jit(solution)/shard_map/ppermute | solution.py:312
  230.9 5.2 %collective-permute-start.28 = (f32[2,64,128]{2,1,0:T(8,128)S(1)}, f32[2,64,128]{2,1,0:T(8,128)S(1)}, u32[]{:S(2)}, u32[]{:S(2)}) collective-permute-start(f32[2,64,128]{2,1,0:T(8,128)S(1)} %add_subtract_fusion), channel_id=1, source_target_pairs={{0,24},{8,16},{16,8},{24,0},{1,25},{9,17},{17,9},{25,1},{2,26},{10... | collective-permute-start | bytes 196616 | tf_op jit(solution)/shard_map/ppermute | solution.py:312
  (4 other events, 52.9 us)
